TPU v7x, 32 devices: a whole 2x2x4 slice. The times are simulated.
32 devices in a mesh: gauss: 16 (over z, x, core), tile: 2 (over y).
Axes of the slice: x: 2, y: 2, z: 4, core: 2. Of those that a mesh axis runs over, the one named last changes fastest.
Arguments:
- splats: float32 [9, 32768], P(None, ('gauss', 'tile')), may hold values from -8 to 260, as said below
- sh_coeffs: float32 [48, 32768], P(None, ('gauss', 'tile')), may hold values from -2 to 2
- send_list: int32 [32768], P(('gauss', 'tile')), may hold values from 0 to 1023, as said below
- block_slots: int32 [16, 96, 128], P('gauss', 'tile'), may hold values from 0 to 1023, as said below
- block_tiles: int32 [16, 96], P('gauss', 'tile'), may hold values from 0 to 8, as said below
- target: float32 [3, 256, 256], P(None, 'gauss', 'tile'), may hold values from 0 to 1
Outputs:
- rendered: float32 [3, 256, 256], P(None, 'gauss', 'tile')
- grad_splats: float32 [9, 32768], P(None, ('gauss', 'tile'))
- grad_sh: float32 [48, 32768], P(None, ('gauss', 'tile'))
Inputs may be any that keep to these rules, and one draw needn't show every extreme that they name: `send_list`: each device's 1024 entries are a permutation of 0 to 1023. `block_tiles`: each device's 48 entries never fall; each of its tiles 0 to 7 has at least one block; the value 8 marks an unused slot; in every draw some device uses all 48 slots. `block_slots`: entries index the device's received Gaussians. `splats`: conics are positive definite; view directions have unit length; opacity logits (row 5) lie between -8 and -2.
All inputs are finite; a program needn't handle non-finite values.
Results may differ from a plain program's by a relative error of at most 0.0003.
Values sent between devices are 32-bit elements; how exact they have to be, the bound alone decides.
A program may use at most 64 MiB of HBM per device.

v0:
```python
import jax
import jax.numpy as jnp
from jax import lax
from jax.sharding import PartitionSpec as P

TILE_SIDE = 16
TILES_DEV = 8


HIGHEST = lax.Precision.HIGHEST
BASE_ZERO = 0.28209479177387814
BASE_ONE = 0.4886025119029199
BASE_TWO = (
    1.0925484305920792,
    -1.0925484305920792,
    0.31539156525252005,
    -1.0925484305920792,
    0.5462742152960396,
)
BASE_THREE = (
    -0.5900435899266435,
    2.890611442640554,
    -0.4570457994644658,
    0.3731763325901154,
    -0.4570457994644658,
    1.445305721320277,
    -0.5900435899266435,
)
CONST_ONE = 0.0001
CONST_TWO = 0.0009


def extended(cells, sides, width):
    for axis, dim in sides:
        count = lax.axis_size(axis)
        ends = count - 1
        head = lax.slice_in_dim(cells, 0, width, axis=dim)
        tail = lax.slice_in_dim(cells, cells.shape[dim] - width, cells.shape[dim], axis=dim)
        cells = jnp.concatenate(
            [
                lax.ppermute(tail, axis, [(i, (i + 1) % count) for i in range(ends)]),
                cells,
                lax.ppermute(head, axis, [((i + 1) % count, i) for i in range(ends)]),
            ],
            axis=dim,
        )
    return cells


def harmonics(direction):
    coord_x, coord_y, coord_z = (direction[0], direction[1], direction[2])
    square_x, square_y, square_z = (coord_x * coord_x, coord_y * coord_y, coord_z * coord_z)
    rows_list = [
        jnp.full_like(coord_x, BASE_ZERO),
        -BASE_ONE * coord_y,
        BASE_ONE * coord_z,
        -BASE_ONE * coord_x,
        BASE_TWO[0] * coord_x * coord_y,
        BASE_TWO[1] * coord_y * coord_z,
        BASE_TWO[2] * (2.0 * square_z - square_x - square_y),
        BASE_TWO[3] * coord_x * coord_z,
        BASE_TWO[4] * (square_x - square_y),
        BASE_THREE[0] * coord_y * (3.0 * square_x - square_y),
        BASE_THREE[1] * coord_x * coord_y * coord_z,
        BASE_THREE[2] * coord_y * (4.0 * square_z - square_x - square_y),
        BASE_THREE[3] * coord_z * (2.0 * square_z - 3.0 * square_x - 3.0 * square_y),
        BASE_THREE[4] * coord_x * (4.0 * square_z - square_x - square_y),
        BASE_THREE[5] * coord_z * (square_x - square_y),
        BASE_THREE[6] * coord_x * (square_x - 3.0 * square_y),
    ]
    return jnp.stack(rows_list)


def shade(direction, coeffs):
    basis = harmonics(direction)
    return 0.5 + jnp.sum(coeffs.reshape(3, 16, -1) * basis[None], axis=1)


def composite(records):
    members = records.shape[1]
    pixels = jnp.arange(TILE_SIDE * TILE_SIDE)
    pixel_u = (pixels % TILE_SIDE).astype(jnp.float32)
    pixel_v = (pixels // TILE_SIDE).astype(jnp.float32)
    delta_x = pixel_u[None, :] - records[0][:, None]
    delta_y = pixel_v[None, :] - records[1][:, None]
    exponent = (
        -0.5 * (records[2][:, None] * delta_x * delta_x + records[4][:, None] * delta_y * delta_y)
        - records[3][:, None] * delta_x * delta_y
    )
    alphas = jax.nn.sigmoid(records[5])[:, None] * jnp.exp(exponent)
    logged = jnp.log1p(-alphas)
    positions = jnp.arange(members)
    earlier_mask = (positions[None, :] < positions[:, None]).astype(jnp.float32)
    before = jnp.dot(earlier_mask, logged, precision=HIGHEST, preferred_element_type=jnp.float32)
    weight = alphas * jnp.exp(before)
    colour = jnp.dot(records[6:9], weight, precision=HIGHEST, preferred_element_type=jnp.float32)
    return jnp.concatenate([colour, jnp.sum(logged, axis=0, keepdims=True)], axis=0)


def block_pullback(paired):
    unused, pulling = jax.vjp(composite, paired[0])
    return pulling(paired[1])[0]


def combine(results, tile_ids):
    positions = jnp.arange(results.shape[0])
    earlier = (
        (tile_ids[:, None] == tile_ids[None, :]) & (positions[None, :] < positions[:, None])
    ).astype(jnp.float32)
    prefix = jnp.dot(earlier, results[:, 3], precision=HIGHEST, preferred_element_type=jnp.float32)
    member = (jnp.arange(TILES_DEV)[:, None] == tile_ids[None, :]).astype(jnp.float32)
    shaded = jnp.exp(prefix)[:, None, :] * results[:, 0:3]
    return jnp.einsum("kb,bcp->kcp", member, shaded, precision=HIGHEST)


def to_image(tiles_img):
    return (
        tiles_img.reshape(TILES_DEV, 3, TILE_SIDE, TILE_SIDE)
        .transpose(1, 2, 0, 3)
        .reshape(3, TILE_SIDE, TILES_DEV * TILE_SIDE)
    )


def window():
    tap_offsets = jnp.arange(11).astype(jnp.float32) - 5.0
    profile = jnp.exp(-tap_offsets * tap_offsets / 4.5)
    return profile / jnp.sum(profile)


def blur(padded, rows_out, cols_out):
    weights = window()
    across = weights[0] * padded[..., :, 0:cols_out]
    for offset in range(1, 11):
        across = across + weights[offset] * padded[..., :, offset : offset + cols_out]
    result = weights[0] * across[..., 0:rows_out, :]
    for offset in range(1, 11):
        result = result + weights[offset] * across[..., offset : offset + rows_out, :]
    return result


def similarity(mu_x, mu_y, sq_x, sq_y, cross_xy):
    mean_xy = mu_x * mu_y
    numerator = (2.0 * mean_xy + CONST_ONE) * (2.0 * (cross_xy - mean_xy) + CONST_TWO)
    denominator = (mu_x * mu_x + mu_y * mu_y + CONST_ONE) * (
        sq_x - mu_x * mu_x + sq_y - mu_y * mu_y + CONST_TWO
    )
    return numerator / denominator


def five_products(padded):
    return jnp.stack(
        [padded[0], padded[1], padded[0] * padded[0], padded[1] * padded[1], padded[0] * padded[1]]
    )


def similarity_grads(moments):

    def partial_loss(mean_x, square_x, product_xy):
        return jnp.sum(
            0.2 * (1.0 - similarity(mean_x, moments[1], square_x, moments[3], product_xy))
        )

    return jnp.stack(jax.grad(partial_loss, argnums=(0, 1, 2))(moments[0], moments[2], moments[4]))


def run_live(apply, arrays_in, live, out_shape):

    def advance(position, buffer):
        picked = tuple(
            (lax.dynamic_index_in_dim(member, position, 0, keepdims=False) for member in arrays_in)
        )
        return lax.dynamic_update_index_in_dim(buffer, apply(picked), position, 0)

    return lax.fori_loop(0, live, advance, jnp.zeros(out_shape, jnp.float32))


def body(splats, sh_coeffs, send_list, block_slots, block_tiles, target):
    row_band = lax.axis_index("gauss")
    col_band = lax.axis_index("tile")
    owners = lax.axis_size("gauss")
    peers = lax.axis_size("tile")
    own_records = jnp.concatenate([splats[0:6], shade(splats[6:9], sh_coeffs)], axis=0)
    received = lax.all_to_all(
        own_records[:, send_list], "gauss", split_axis=1, concat_axis=1, tiled=True
    )
    tile_ids = block_tiles[0]
    slot_rows = block_slots[0]
    slots_total = slot_rows.shape[0]
    gathered = received[:, slot_rows.reshape(-1)].reshape(9, slots_total, slot_rows.shape[1])
    anchor_x = (TILE_SIDE * (TILES_DEV * col_band + jnp.minimum(tile_ids, TILES_DEV - 1))).astype(
        jnp.float32
    )
    anchor_y = (TILE_SIDE * row_band).astype(jnp.float32)
    shifted = jnp.concatenate(
        [gathered[0:1] - anchor_x[None, :, None], gathered[1:2] - anchor_y, gathered[2:9]], axis=0
    )
    per_block = jnp.moveaxis(shifted, 1, 0)
    live = jnp.sum((tile_ids < TILES_DEV).astype(jnp.int32))
    pixel_count = TILE_SIDE * TILE_SIDE
    results = run_live(
        lambda picked: composite(picked[0]), (per_block,), live, (slots_total, 4, pixel_count)
    )
    tiles_img = combine(results, tile_ids)
    rendered = to_image(tiles_img)
    rows_here = rendered.shape[1]
    cols_here = rendered.shape[2]
    padded = extended(jnp.stack([rendered, target]), (("gauss", 2), ("tile", 3)), 10)
    moments = blur(five_products(padded), rows_here + 10, cols_here + 10)
    grads_map = similarity_grads(moments)
    row_ids = row_band * rows_here - 5 + jnp.arange(rows_here + 10)
    col_ids = col_band * cols_here - 5 + jnp.arange(cols_here + 10)
    inside = ((row_ids >= 0) & (row_ids < rows_here * owners))[:, None] & (
        (col_ids >= 0) & (col_ids < cols_here * peers)
    )[None, :]
    spread = blur(grads_map * inside.astype(jnp.float32), rows_here, cols_here)
    pixel_grad = (
        spread[0] + 2.0 * rendered * spread[1] + target * spread[2] + 1.6 * (rendered - target)
    )
    tile_grad = (
        pixel_grad.reshape(3, TILE_SIDE, TILES_DEV, TILE_SIDE)
        .transpose(2, 0, 1, 3)
        .reshape(TILES_DEV, 3, pixel_count)
    )
    unused, combine_pull = jax.vjp(lambda found: combine(found, tile_ids), results)
    results_grad = combine_pull(tile_grad)[0]
    block_grad = run_live(block_pullback, (per_block, results_grad), live, per_block.shape)
    flat_grad = jnp.moveaxis(block_grad, 0, 1).reshape(9, -1)
    table_grad = jnp.zeros_like(received).at[:, slot_rows.reshape(-1)].add(flat_grad)
    back_records = lax.all_to_all(table_grad, "gauss", split_axis=1, concat_axis=1, tiled=True)
    own_grad = jnp.zeros_like(own_records).at[:, send_list].set(back_records)
    unused_colour, shade_pull = jax.vjp(shade, splats[6:9], sh_coeffs)
    dir_grad, grad_sh = shade_pull(own_grad[6:9])
    grad_splats = jnp.concatenate([own_grad[0:6], dir_grad], axis=0)
    return (rendered, grad_splats, grad_sh)


def solution(mesh):
    in_specs = (
        P(None, ("gauss", "tile")),
        P(None, ("gauss", "tile")),
        P(("gauss", "tile")),
        P("gauss", "tile", None),
        P("gauss", "tile"),
        P(None, "gauss", "tile"),
    )
    out_specs = (P(None, "gauss", "tile"), P(None, ("gauss", "tile")), P(None, ("gauss", "tile")))
    return jax.shard_map(body, mesh=mesh, in_specs=in_specs, out_specs=out_specs, check_vma=False)
```

profile of v0, /device:TPU:0, one launch (start us, length us, event | category | flops | bytes accessed | tf_op | source)
XLA Modules:
  0.0 364.5 jit_solution(15220192069105559157)
XLA Ops:
  0.6 0.9 multiply_multiply_fusion.2
  1.5 0.8 slice.409
  2.3 0.9 multiply_multiply_fusion.3
  3.3 1.0 multiply_reduce_fusion.2
  4.6 0.7 compare_select_fusion.1
  5.3 2.8 gather_fusion
  8.3 0.7 reshape.453
  9.0 7.4 %all-to-all-start = ((f32[16,1,576]{2,1,0:T(1,128)}), f32[16,1,576]{2,1,0:T(1,128)S(1)}, u32[]{:S(2)}, u32[]{:S(2)}) async-start(f32[16,1,576]{2,1,0:T(1,128)} %reshape.453), calls=%async_computation | async-start | bytes 81920 | tf_op jit(solution)/shard_map/all_to_all | solution.py:183
  16.4 0.8 compare_select_fusion
  17.3 1.4 multiply_convert_fusion
  18.7 0.6 fusion.158
  19.3 3.8 %all-to-all-done = f32[16,1,576]{2,1,0:T(1,128)S(1)} async-done(((f32[16,1,576]{2,1,0:T(1,128)}), f32[16,1,576]{2,1,0:T(1,128)S(1)}, u32[]{:S(2)}, u32[]{:S(2)}) %all-to-all-start) | async-done | bytes 36896 | tf_op jit(solution)/shard_map/all_to_all | solution.py:183
  23.1 0.5 broadcast.786
  23.6 0.7 reduce.4
  24.5 1.0 copy.59
  25.5 17.1 %gather_fusion.1 = f32[6144,9]{1,0:T(8,128)S(1)} fusion(f32[9,1024]{0,1:T(8,128)} %bitcast.194, s32[6144]{0:T(1024)S(1)} %broadcast_clamp_fusion), kind=kCustom, calls=%fused_computation.1 | custom fusion | bytes 466944 | tf_op jit(solution)/shard_map/gather | solution.py:189
  42.6 2.5 slice.497
  45.2 2.5 slice_reduce_fusion
  47.7 2.4 copy.62
  50.3 39.1 %while.24 = (s32[]{:T(128)}, f32[48,4,256]{2,1,0:T(4,128)S(1)}, s32[]{:T(128)}, f32[48,9,128]{2,1,0:T(8,128)S(1)}, s32[]{:T(128)}, /*index=5*/s32[]{:T(128)}, s3...) while((s32[]{:T(128)}, f32[48,4,256]{2,1,0:T(4,128)S(1)}, s32[]{:T(128)}, f32[48,9,128]{2,1,0:T(8,128)S(1)}, ...), condition=%wide.region_4.5_spmd, body=%wide.region_2.4_spmd.sunk | while | flops 52843144 | bytes 296203 | solution.py:174
  90.3 1.3 collective-permute-start
  91.6 1.3 collective-permute-start.1
  92.9 0.6 broadcast_divide_fusion
  93.5 1.2 collective-permute-done.1
  94.8 2.4 collective-permute-start.2
  97.2 1.3 collective-permute-start.3
  98.5 0.7 fusion.161
  99.6 4.4 %collective-permute-done.3 = f32[2,3,36,10]{3,2,1,0:T(8,128)S(1)} collective-permute-done((f32[2,3,36,10]{3,2,1,0:T(8,128)S(1)}, f32[2,3,36,10]{3,2,1,0:T(8,128)S(1)}, u32[]{:S(2)}, u32[]{:S(2)}) %collective-permute-start.3) | collective-permute-done | bytes 8672 | tf_op jit(solution)/shard_map/ppermute | solution.py:43
  104.4 8.4 %fusion.74 = f32[5,3,36,138]{3,2,1,0:T(8,128)S(1)} fusion(f32[5,3,36,148]{3,2,1,0:T(8,128)S(1)} %pad_maximum_fusion, f32[]{:T(128)} %bitcast.51, f32[]{:T(128)} %bitcast.50, f32[]{:T(128)} %bitcast.49, f32[]{:T(128)} %bitcast.48, f32[]{:T(128)} %bitcast.47, f32[]{:T(128)} %bitcast.46, f32[]{:T(128)} %bitcast.45, f32[]{:T(128)} %bitcast.44, f32[]{:T(128)} %bitcast.43, ...), kind=kLoop, calls=%fused_computation.138 | loop fusion | flops 1564920 | bytes 3577004 | tf_op jit(solution)/shard_map/add | solution.py:134
  112.8 7.4 %fusion.84 = f32[5,3,26,138]{3,2,1,0:T(8,128)S(1)} fusion(f32[5,3,36,138]{3,2,1,0:T(8,128)S(1)} %fusion.74, f32[]{:T(128)} %bitcast.51, f32[]{:T(128)} %bitcast.50, f32[]{:T(128)} %bitcast.49, f32[]{:T(128)} %bitcast.48, f32[]{:T(128)} %bitcast.47, f32[]{:T(128)} %bitcast.46, f32[]{:T(128)} %bitcast.45, f32[]{:T(128)} %bitcast.44, f32[]{:T(128)} %bitcast.43, ...), kind=kLoop, calls=%fused_computation.160 | loop fusion | flops 1130220 | bytes 2583404 | tf_op jit(solution)/shard_map/add | solution.py:137
  120.5 7.2 %fusion.98 = f32[3,3,26,128]{3,2,1,0:T(8,128)S(1)} fusion(f32[3,3,26,138]{3,2,1,0:T(8,128)S(1)} %maximum_multiply_fusion, f32[]{:T(128)} %bitcast.51, f32[]{:T(128)} %bitcast.50, f32[]{:T(128)} %bitcast.49, f32[]{:T(128)} %bitcast.48, f32[]{:T(128)} %bitcast.47, f32[]{:T(128)} %bitcast.46, f32[]{:T(128)} %bitcast.45, f32[]{:T(128)} %bitcast.44, ...), kind=kLoop, calls=%fused_computation.193 | loop fusion | flops 628992 | bytes 1437740 | tf_op jit(solution)/shard_map/add | solution.py:134
  127.7 6.9 %fusion.117 = f32[3,3,16,128]{3,2,1,0:T(8,128)S(1)} fusion(f32[3,3,26,128]{3,2,1,0:T(8,128)S(1)} %fusion.98, f32[]{:T(128)} %bitcast.51, f32[]{:T(128)} %bitcast.50, f32[]{:T(128)} %bitcast.49, f32[]{:T(128)} %bitcast.48, f32[]{:T(128)} %bitcast.47, f32[]{:T(128)} %bitcast.46, f32[]{:T(128)} %bitcast.45, f32[]{:T(128)} %bitcast.44, f32[]{:T(128)} %bitcast.43, ...), kind=kLoop, calls=%fused_computation.238 | loop fusion | flops 387072 | bytes 884780 | tf_op jit(solution)/shard_map/add | solution.py:137
  135.6 68.4 %while.25 = (s32[]{:T(128)}, f32[48,9,128]{2,1,0:T(8,128)S(1)}, s32[]{:T(128)}, f32[48,4,256]{2,0,1:T(8,128)S(1)}, f32[48,9,128]{2,1,0:T(8,128)S(1)}, /*index=5*...) while((s32[]{:T(128)}, f32[48,9,128]{2,1,0:T(8,128)S(1)}, ...), condition=%wide.region_14.15_spmd, body=%wide.region_7.0_spmd.sunk | while | flops 106244616 | bytes 1247007 | solution.py:174
  137.3 0.4 multiply_multiply_fusion.12
  140.1 0.4 multiply_multiply_fusion.12
  142.9 0.4 multiply_multiply_fusion.12
  145.8 0.4 multiply_multiply_fusion.12
  148.6 0.4 multiply_multiply_fusion.12
  151.4 0.4 multiply_multiply_fusion.12
  154.2 0.4 multiply_multiply_fusion.12
  204.2 1.1 copy.69
  205.3 34.3 %scatter_custom_fusion = f32[9,1024]{0,1:T(8,128)} fusion(s32[6144]{0:T(1024)} %bitcast.222, f32[6144,9]{1,0:T(8,128)S(1)} %copy.69, f32[]{:T(128)} %constant.207.clone.1), kind=kCustom, calls=%fused_computation.184 | custom fusion | flops 55296 | bytes 37376 | tf_op jit(solution)/shard_map/scatter-add | solution.py:228
  239.6 1.3 copy.70
  240.9 117.0 %all_to_all.24 = f32[16,1,576]{2,1,0:T(1,128)S(1)} all-to-all(f32[16,1,576]{2,1,0:T(1,128)S(1)} %reshape.455), channel_id=1, replica_groups=mesh['gauss'=16,'tile'=2] {'gauss'}, dimensions={0} | all-to-all | bytes 73728 | tf_op jit(solution)/shard_map/all_to_all | solution.py:229
  357.9 0.7 reduce.5
  359.1 3.2 scatter_custom_fusion.1
  362.7 0.7 broadcast_multiply_fusion
  363.9 0.6 pad_maximum_fusion.4
  (521 shorter events, 71.6 us)
Async XLA Ops:
  3.3 1.0 copy-start.2
  9.0 14.1 %all-to-all-start = ((f32[16,1,576]{2,1,0:T(1,128)}), f32[16,1,576]{2,1,0:T(1,128)S(1)}, u32[]{:S(2)}, u32[]{:S(2)}) async-start(f32[16,1,576]{2,1,0:T(1,128)} %reshape.453), calls=%async_computation | async-start | bytes 81920 | tf_op jit(solution)/shard_map/all_to_all | solution.py:183
  17.2 6.4 %copy-start.6 = (s32[6144,1]{0,1:T(1,128)}, s32[6144,1]{0,1:T(1,128)S(1)}, u32[]{:S(2)}) copy-start(s32[6144,1]{0,1:T(1,128)S(1)} %compare_select_fusion) | copy-start | bytes 73732
  50.3 39.2 %copy-start.7 = (s32[1,48]{1,0:T(1,128)S(1)}, s32[1,48]{1,0:T(1,128)}, u32[]{:S(2)}) copy-start(s32[1,48]{1,0:T(1,128)} %param.14) | copy-start | bytes 580
  50.3 40.0 %copy-start.1 = (f32[3,16,128]{2,1,0:T(8,128)S(1)}, f32[3,16,128]{2,1,0:T(8,128)}, u32[]{:S(2)}) copy-start(f32[3,16,128]{2,1,0:T(8,128)} %param.15) | copy-start | bytes 73732
  90.3 3.2 collective-permute-start
  91.6 3.1 collective-permute-start.1
  94.8 4.8 %collective-permute-start.2 = (f32[2,3,36,10]{3,2,1,0:T(8,128)S(1)}, f32[2,3,36,10]{3,2,1,0:T(8,128)S(1)}, u32[]{:S(2)}, u32[]{:S(2)}) collective-permute-start(f32[2,3,36,10]{3,2,1,0:T(8,128)S(1)} %get-tuple-element.216), channel_id=1, source_target_pairs={{0,1},{2,3},{4,5},{6,7},{8,9},{10,11},{12,13},{14,15},{16,17},{18,... | collective-permute-start | bytes 25928 | tf_op jit(solution)/shard_map/ppermute | solution.py:41
  97.2 6.8 %collective-permute-start.3 = (f32[2,3,36,10]{3,2,1,0:T(8,128)S(1)}, f32[2,3,36,10]{3,2,1,0:T(8,128)S(1)}, u32[]{:S(2)}, u32[]{:S(2)}) collective-permute-start(f32[2,3,36,10]{3,2,1,0:T(8,128)S(1)} %get-tuple-element.217), channel_id=1, source_target_pairs={{1,0},{3,2},{5,4},{7,6},{9,8},{11,10},{13,12},{15,14},{17,16},{19,... | collective-permute-start | bytes 25928 | tf_op jit(solution)/shard_map/ppermute | solution.py:43
  99.3 35.3 %copy-start.5 = (f32[3,16,128]{2,1,0:T(8,128)}, f32[3,16,128]{2,1,0:T(8,128)S(1)}, u32[]{:S(2)}) copy-start(f32[3,16,128]{2,1,0:T(8,128)S(1)} %reshape.407) | copy-start | bytes 73732
  205.3 157.4 %copy-start = (f32[48,1024]{1,0:T(8,128)S(1)}, f32[48,1024]{1,0:T(8,128)}, u32[]{:S(2)}) copy-start(f32[48,1024]{1,0:T(8,128)} %param.11) | copy-start | bytes 589828
  205.3 157.4 %copy-start.3 = (f32[16,1024]{1,0:T(8,128)S(1)}, f32[16,1024]{1,0:T(8,128)}, u32[]{:S(2)}) copy-start(f32[16,1024]{1,0:T(8,128)} %copy-done.2) | copy-start | bytes 196612
  205.3 158.1 %copy-start.4 = (f32[9,1024]{1,0:T(8,128)S(1)}, f32[9,1024]{1,0:T(8,128)}, u32[]{:S(2)}) copy-start(f32[9,1024]{1,0:T(8,128)} %param.10) | copy-start | bytes 110596
where the time goes:
time: 367 us; the launch traced here: 365 us
  blocking collectives  117 us (32%)
  other arithmetic  96.1 us (26%)
  matrix products  51.1 us (14%)
  loops' own time  38.3 us (10%)
  local copies, waits for them, and re-layouts  37.7 us (10%)
  starting transfers between devices  13.6 us (4%)
  waiting for transfers between devices  9.67 us (3%)
    all_to_all x1, blocking collectives, body(): lax.all_to_all(table_grad, 'gauss', split_axis=1, concat_axis=1, tiled=True)  117 us
    another operation x2, loops' own time, run_live(): return lax.fori_loop(0, live, advance, jnp.zeros(out_shape, jnp.float32))  38.3 us
    scatter-add x1, other arithmetic, body(): jnp.zeros_like(received).at[:, slot_rows.reshape(-1)].add(flat_grad)  34.3 us
    dot_general x72, matrix products, composite(): jnp.dot(earlier_mask, logged, precision=HIGHEST, preferred_element_type=j...  30.9 us
    dot_general x72, matrix products, composite(): jnp.dot(records[6:9], weight, precision=HIGHEST, preferred_element_type=j...  19.2 us
    gather x1, local copies, waits for them, and re-layouts, body(): received[:, slot_rows.reshape(-1)]  17.1 us
    add x2, other arithmetic, blur(): across = across + weights[offset] * padded[..., :, offset:offset + cols_out]  15.7 us
    add x2, other arithmetic, blur(): result = result + weights[offset] * across[..., offset:offset + rows_out, :]  14.3 us
  transfers between devices with their start and end apart: 5, of which 4 were waited for; matrix products, arithmetic and copies ran while one was open for 1% of the time, Pallas kernels for 0%

commit v1 on v0

--- a/solution.py
+++ b/solution.py
@@ -1,6 +1,8 @@
 import jax
 import jax.numpy as jnp
 from jax import lax
+from jax.experimental import pallas as pl
+from jax.experimental.pallas import tpu as pltpu
 from jax.sharding import PartitionSpec as P
 
 TILE_SIDE = 16
@@ -76,41 +78,301 @@
     return 0.5 + jnp.sum(coeffs.reshape(3, 16, -1) * basis[None], axis=1)
 
 
-def composite(records):
-    members = records.shape[1]
-    pixels = jnp.arange(TILE_SIDE * TILE_SIDE)
-    pixel_u = (pixels % TILE_SIDE).astype(jnp.float32)
-    pixel_v = (pixels // TILE_SIDE).astype(jnp.float32)
-    delta_x = pixel_u[None, :] - records[0][:, None]
-    delta_y = pixel_v[None, :] - records[1][:, None]
-    exponent = (
-        -0.5 * (records[2][:, None] * delta_x * delta_x + records[4][:, None] * delta_y * delta_y)
-        - records[3][:, None] * delta_x * delta_y
-    )
-    alphas = jax.nn.sigmoid(records[5])[:, None] * jnp.exp(exponent)
-    logged = jnp.log1p(-alphas)
-    positions = jnp.arange(members)
-    earlier_mask = (positions[None, :] < positions[:, None]).astype(jnp.float32)
-    before = jnp.dot(earlier_mask, logged, precision=HIGHEST, preferred_element_type=jnp.float32)
-    weight = alphas * jnp.exp(before)
-    colour = jnp.dot(records[6:9], weight, precision=HIGHEST, preferred_element_type=jnp.float32)
-    return jnp.concatenate([colour, jnp.sum(logged, axis=0, keepdims=True)], axis=0)
-
-
-def block_pullback(paired):
-    unused, pulling = jax.vjp(composite, paired[0])
-    return pulling(paired[1])[0]
-
-
-def combine(results, tile_ids):
-    positions = jnp.arange(results.shape[0])
-    earlier = (
-        (tile_ids[:, None] == tile_ids[None, :]) & (positions[None, :] < positions[:, None])
-    ).astype(jnp.float32)
-    prefix = jnp.dot(earlier, results[:, 3], precision=HIGHEST, preferred_element_type=jnp.float32)
-    member = (jnp.arange(TILES_DEV)[:, None] == tile_ids[None, :]).astype(jnp.float32)
-    shaded = jnp.exp(prefix)[:, None, :] * results[:, 0:3]
-    return jnp.einsum("kb,bcp->kcp", member, shaded, precision=HIGHEST)
+SEGMENTS = 8
+STEPS = 16
+BLOCK = SEGMENTS * STEPS
+HALF = 128
+CENTRE = 7.5
+CHUNK = 256
+
+
+def selector(slots_row, base, rows):
+    rows_at = lax.broadcasted_iota(jnp.int32, (rows, slots_row.shape[1]), 0) + base
+    return jnp.where(rows_at == slots_row, 1.0, 0.0).astype(jnp.bfloat16)
+
+
+def halves(value):
+    high = value.astype(jnp.bfloat16)
+    low = (value - high.astype(jnp.float32)).astype(jnp.bfloat16)
+    return high, low
+
+
+def pixel_axes():
+    lanes = lax.broadcasted_iota(jnp.int32, (SEGMENTS, HALF), 1)
+    along = (lanes % TILE_SIDE).astype(jnp.float32) - CENTRE
+    down = (lanes // TILE_SIDE).astype(jnp.float32) - CENTRE
+    return along, (down, down + float(HALF // TILE_SIDE))
+
+
+def columns_of(col_ref, step):
+    sub = col_ref[step * SEGMENTS : (step + 1) * SEGMENTS, :]
+    return [jnp.broadcast_to(sub[:, k : k + 1], (SEGMENTS, HALF)) for k in range(9)]
+
+
+def alphas_of(cols, along, down):
+    delta_x = along - cols[0]
+    delta_y = down - cols[1]
+    exponent = cols[2] * delta_x * delta_x + delta_y * (cols[3] * delta_x + cols[4] * delta_y)
+    return cols[5] * jnp.exp(exponent)
+
+
+def forward_kernel(
+    tile_ref, info_ref, recv_ref, slots_ref, image_ref, rec_ref, saved_ref, pad_ref, split_ref, col_ref
+):
+    live = info_ref[0]
+    own = recv_ref.shape[1]
+    pad_ref[...] = jnp.zeros_like(pad_ref)
+    pad_ref[0:9, :] = recv_ref[...]
+    whole = pad_ref[...]
+    first = whole.astype(jnp.bfloat16)
+    rest = whole - first.astype(jnp.float32)
+    second = rest.astype(jnp.bfloat16)
+    third = (rest - second.astype(jnp.float32)).astype(jnp.bfloat16)
+    split_ref[0:16, :] = first
+    split_ref[16:32, :] = second
+    split_ref[32:48, :] = third
+    row_at = lax.broadcasted_iota(jnp.int32, (16, BLOCK), 0)
+    base_y = info_ref[2].astype(jnp.float32) + CENTRE
+
+    def collect(pair, carry):
+        slots_row = slots_ref[pl.ds(pair, 1), :]
+        found = jnp.zeros((48, 2 * BLOCK), jnp.float32)
+        for base in range(0, own, CHUNK):
+            found = found + jnp.dot(
+                split_ref[:, base : base + CHUNK],
+                selector(slots_row, base, CHUNK),
+                preferred_element_type=jnp.float32,
+            )
+        joined = found[0:16] + found[16:32] + found[32:48]
+        for side in range(2):
+            slot = 2 * pair + side
+            rec = joined[:, side * BLOCK : (side + 1) * BLOCK]
+            tile = jnp.minimum(tile_ref[slot], TILES_DEV - 1)
+            base_x = (info_ref[1] + TILE_SIDE * tile).astype(jnp.float32) + CENTRE
+            shift = jnp.where(row_at == 0, base_x, jnp.where(row_at == 1, base_y, 0.0))
+            scale = jnp.where(
+                row_at == 3, -1.0, jnp.where((row_at == 2) | (row_at == 4), -0.5, 1.0)
+            )
+            shown = jnp.where(row_at == 5, 1.0 / (1.0 + jnp.exp(-rec)), (rec - shift) * scale)
+            rec_ref[slot] = shown
+        return carry
+
+    lax.fori_loop(0, (live + 1) // 2, collect, 0)
+    along, downs = pixel_axes()
+    seg_at = lax.broadcasted_iota(jnp.int32, (SEGMENTS, HALF), 0)
+
+    def draw(slot, carry):
+        tile = tile_ref[slot]
+        fresh = (slot == 0) | (tile != tile_ref[jnp.maximum(slot - 1, 0)])
+        col_ref[...] = jnp.transpose(rec_ref[slot])
+        through = [jnp.ones((SEGMENTS, HALF), jnp.float32) for side in range(2)]
+        sums = [[jnp.zeros((SEGMENTS, HALF), jnp.float32) for c in range(3)] for side in range(2)]
+        for step in range(STEPS):
+            cols = columns_of(col_ref, step)
+            for side in range(2):
+                weight = alphas_of(cols, along, downs[side]) * through[side]
+                through[side] = through[side] - weight
+                for c in range(3):
+                    sums[side][c] = sums[side][c] + cols[6 + c] * weight
+        after = []
+        for side in range(2):
+            start = jnp.where(fresh, 1.0, carry[side])
+            running = through[side]
+            for shift in (1, 2, 4):
+                running = jnp.where(
+                    seg_at >= shift, running * pltpu.roll(running, shift, 0), running
+                )
+            before = jnp.where(seg_at == 0, 1.0, pltpu.roll(running, 1, 0)) * start
+            after.append(start * running[SEGMENTS - 1 : SEGMENTS])
+            lanes = slice(side * HALF, (side + 1) * HALF)
+            saved_ref[slot, 0, :, lanes] = before
+            saved_ref[slot, 1, :, lanes] = through[side]
+            for c in range(3):
+                saved_ref[slot, 2 + c, :, lanes] = sums[side][c]
+                shade_sum = jnp.sum(before * sums[side][c], axis=0, keepdims=True)
+                held = jnp.where(fresh, 0.0, image_ref[tile, c : c + 1, lanes])
+                image_ref[tile, c : c + 1, lanes] = held + shade_sum
+        return tuple(after)
+
+    ones = jnp.ones((1, HALF), jnp.float32)
+    lax.fori_loop(0, live, draw, (ones, ones))
+
+
+def backward_kernel(
+    tile_ref, info_ref, rec_ref, saved_ref, grad_ref, slots_ref, out_ref,
+    col_ref, weight_ref, pull_ref, block_ref, acc_ref,
+):
+    live = info_ref[0]
+    own = out_ref.shape[1]
+    slots_total = rec_ref.shape[0]
+    block_ref[...] = jnp.zeros_like(block_ref)
+    acc_ref[...] = jnp.zeros_like(acc_ref)
+    along, downs = pixel_axes()
+    seg_at = lax.broadcasted_iota(jnp.int32, (SEGMENTS, HALF), 0)
+    rows16 = lax.broadcasted_iota(jnp.int32, (16, 2 * HALF), 0)
+    pixels = lax.broadcasted_iota(jnp.int32, (16, 2 * HALF), 1)
+    wide_u = (pixels % TILE_SIDE).astype(jnp.float32) - CENTRE
+    wide_v = (pixels // TILE_SIDE).astype(jnp.float32) - CENTRE
+    basis = jnp.zeros((16, 2 * HALF), jnp.float32)
+    for at, term in enumerate(
+        (jnp.ones_like(wide_u), wide_u, wide_v, wide_u * wide_u, wide_u * wide_v, wide_v * wide_v)
+    ):
+        basis = jnp.where(rows16 == at, term, basis)
+    basis = basis.astype(jnp.bfloat16)
+    across = (((1,), (1,)), ((), ()))
+
+    def pull(turn, carry):
+        slot = live - 1 - turn
+        tile = tile_ref[slot]
+        final = (turn == 0) | (tile != tile_ref[jnp.minimum(slot + 1, slots_total - 1)])
+        rec = rec_ref[slot]
+        col_ref[...] = jnp.transpose(rec)
+        grads = grad_ref[tile]
+        after = []
+        behind = []
+        through = []
+        colour_g = []
+        for side in range(2):
+            lanes = slice(side * HALF, (side + 1) * HALF)
+            start = jnp.where(final, 0.0, carry[side])
+            tints = [jnp.broadcast_to(grads[c : c + 1, lanes], (SEGMENTS, HALF)) for c in range(3)]
+            colour_g.append(tints)
+            total = tints[0] * saved_ref[slot, 2, :, lanes]
+            for c in (1, 2):
+                total = total + tints[c] * saved_ref[slot, 2 + c, :, lanes]
+            factor = saved_ref[slot, 1, :, lanes]
+            for shift in (1, 2, 4):
+                inside = seg_at < SEGMENTS - shift
+                total = jnp.where(
+                    inside, total + factor * pltpu.roll(total, SEGMENTS - shift, 0), total
+                )
+                factor = jnp.where(
+                    inside, factor * pltpu.roll(factor, SEGMENTS - shift, 0), factor
+                )
+            entering = total + factor * start
+            after.append(entering[0:1])
+            behind.append(
+                jnp.where(seg_at < SEGMENTS - 1, pltpu.roll(entering, SEGMENTS - 1, 0), start)
+            )
+            through.append(saved_ref[slot, 0, :, lanes])
+        alphas = [[], []]
+        weights = [[], []]
+        for step in range(STEPS):
+            cols = columns_of(col_ref, step)
+            for side in range(2):
+                alpha = alphas_of(cols, along, downs[side])
+                weight = alpha * through[side]
+                through[side] = through[side] - weight
+                alphas[side].append(alpha)
+                weights[side].append(weight)
+                lanes = slice(side * HALF, (side + 1) * HALF)
+                weight_ref[step * SEGMENTS : (step + 1) * SEGMENTS, lanes] = weight
+        for step in reversed(range(STEPS)):
+            cols = columns_of(col_ref, step)
+            for side in range(2):
+                lanes = slice(side * HALF, (side + 1) * HALF)
+                tints = colour_g[side]
+                lit = tints[0] * cols[6] + tints[1] * cols[7] + tints[2] * cols[8]
+                gap = lit - behind[side]
+                behind[side] = behind[side] + alphas[side][step] * gap
+                pull_ref[step * SEGMENTS : (step + 1) * SEGMENTS, lanes] = (
+                    weights[side][step] * gap
+                )
+        found = lax.dot_general(
+            basis,
+            jnp.concatenate(halves(pull_ref[...]), axis=0),
+            across,
+            preferred_element_type=jnp.float32,
+        )
+        moment = found[:, :BLOCK] + found[:, BLOCK:]
+        painted = lax.dot_general(
+            jnp.concatenate(halves(grads), axis=0),
+            jnp.concatenate(halves(weight_ref[...]), axis=0),
+            across,
+            preferred_element_type=jnp.float32,
+        )
+        painted = painted[0:8] + painted[8:16]
+        painted = painted[:, :BLOCK] + painted[:, BLOCK:]
+        m_0, m_x, m_y, m_xx, m_xy, m_yy = [moment[k : k + 1] for k in range(6)]
+        at_x, at_y, con_a, con_b, con_c, open_s = [rec[k : k + 1] for k in range(6)]
+        h_x = m_x - at_x * m_0
+        h_y = m_y - at_y * m_0
+        h_xx = m_xx - 2.0 * at_x * m_x + at_x * at_x * m_0
+        h_xy = m_xy - at_x * m_y - at_y * m_x + at_x * at_y * m_0
+        h_yy = m_yy - 2.0 * at_y * m_y + at_y * at_y * m_0
+        block_ref[slot, 0:1, :] = -2.0 * con_a * h_x - con_b * h_y
+        block_ref[slot, 1:2, :] = -2.0 * con_c * h_y - con_b * h_x
+        block_ref[slot, 2:3, :] = -0.5 * h_xx
+        block_ref[slot, 3:4, :] = -h_xy
+        block_ref[slot, 4:5, :] = -0.5 * h_yy
+        block_ref[slot, 5:6, :] = (1.0 - open_s) * m_0
+        block_ref[slot, 6:9, :] = painted[0:3]
+        return tuple(after)
+
+    zeros = jnp.zeros((1, HALF), jnp.float32)
+    lax.fori_loop(0, live, pull, (zeros, zeros))
+
+    def spread(pair, carry):
+        slots_row = slots_ref[pl.ds(pair, 1), :]
+        both = jnp.concatenate([block_ref[2 * pair], block_ref[2 * pair + 1]], axis=1)
+        parts = jnp.concatenate(halves(both), axis=0)
+        for base in range(0, own, CHUNK):
+            lanes = slice(base, base + CHUNK)
+            acc_ref[:, lanes] += lax.dot_general(
+                parts, selector(slots_row, base, CHUNK), across, preferred_element_type=jnp.float32
+            )
+        return carry
+
+    lax.fori_loop(0, (live + 1) // 2, spread, 0)
+    out_ref[...] = acc_ref[0:9, :] + acc_ref[16:25, :]
+
+
+def smem():
+    return pl.BlockSpec(memory_space=pltpu.SMEM)
+
+
+def vmem():
+    return pl.BlockSpec(memory_space=pltpu.VMEM)
+
+
+def draw_tiles(tile_ids, info, received, pairs, slots_total):
+    own = received.shape[1]
+    side = TILE_SIDE * TILE_SIDE
+    return pl.pallas_call(
+        forward_kernel,
+        out_shape=(
+            jax.ShapeDtypeStruct((TILES_DEV, 8, side), jnp.float32),
+            jax.ShapeDtypeStruct((slots_total, 16, BLOCK), jnp.float32),
+            jax.ShapeDtypeStruct((slots_total, 5, SEGMENTS, side), jnp.float32),
+        ),
+        in_specs=[smem(), smem(), vmem(), vmem()],
+        out_specs=(vmem(), vmem(), vmem()),
+        scratch_shapes=[
+            pltpu.VMEM((16, own), jnp.float32),
+            pltpu.VMEM((48, own), jnp.bfloat16),
+            pltpu.VMEM((BLOCK, 16), jnp.float32),
+        ],
+        name="draw_tiles",
+    )(tile_ids, info, received, pairs)
+
+
+def pull_tiles(tile_ids, info, recs, saved, grads, pairs, own):
+    slots_total = recs.shape[0]
+    side = TILE_SIDE * TILE_SIDE
+    return pl.pallas_call(
+        backward_kernel,
+        out_shape=jax.ShapeDtypeStruct((9, own), jnp.float32),
+        in_specs=[smem(), smem(), vmem(), vmem(), vmem(), vmem()],
+        out_specs=vmem(),
+        scratch_shapes=[
+            pltpu.VMEM((BLOCK, 16), jnp.float32),
+            pltpu.VMEM((BLOCK, side), jnp.float32),
+            pltpu.VMEM((BLOCK, side), jnp.float32),
+            pltpu.VMEM((slots_total, 16, BLOCK), jnp.float32),
+            pltpu.VMEM((32, own), jnp.float32),
+        ],
+        name="pull_tiles",
+    )(tile_ids, info, recs, saved, grads, pairs)
 
 
 def to_image(tiles_img):
@@ -163,17 +425,6 @@
     return jnp.stack(jax.grad(partial_loss, argnums=(0, 1, 2))(moments[0], moments[2], moments[4]))
 
 
-def run_live(apply, arrays_in, live, out_shape):
-
-    def advance(position, buffer):
-        picked = tuple(
-            (lax.dynamic_index_in_dim(member, position, 0, keepdims=False) for member in arrays_in)
-        )
-        return lax.dynamic_update_index_in_dim(buffer, apply(picked), position, 0)
-
-    return lax.fori_loop(0, live, advance, jnp.zeros(out_shape, jnp.float32))
-
-
 def body(splats, sh_coeffs, send_list, block_slots, block_tiles, target):
     row_band = lax.axis_index("gauss")
     col_band = lax.axis_index("tile")
@@ -186,21 +437,16 @@
     tile_ids = block_tiles[0]
     slot_rows = block_slots[0]
     slots_total = slot_rows.shape[0]
-    gathered = received[:, slot_rows.reshape(-1)].reshape(9, slots_total, slot_rows.shape[1])
-    anchor_x = (TILE_SIDE * (TILES_DEV * col_band + jnp.minimum(tile_ids, TILES_DEV - 1))).astype(
-        jnp.float32
-    )
-    anchor_y = (TILE_SIDE * row_band).astype(jnp.float32)
-    shifted = jnp.concatenate(
-        [gathered[0:1] - anchor_x[None, :, None], gathered[1:2] - anchor_y, gathered[2:9]], axis=0
-    )
-    per_block = jnp.moveaxis(shifted, 1, 0)
     live = jnp.sum((tile_ids < TILES_DEV).astype(jnp.int32))
     pixel_count = TILE_SIDE * TILE_SIDE
-    results = run_live(
-        lambda picked: composite(picked[0]), (per_block,), live, (slots_total, 4, pixel_count)
-    )
-    tiles_img = combine(results, tile_ids)
+    info = jnp.stack([live, TILE_SIDE * TILES_DEV * col_band, TILE_SIDE * row_band]).astype(jnp.int32)
+    pairs = (
+        slot_rows.reshape(slots_total, SEGMENTS, STEPS)
+        .transpose(0, 2, 1)
+        .reshape(slots_total // 2, 2 * BLOCK)
+    )
+    tiles_img, recs, saved = draw_tiles(tile_ids, info, received, pairs, slots_total)
+    tiles_img = tiles_img[:, 0:3]
     rendered = to_image(tiles_img)
     rows_here = rendered.shape[1]
     cols_here = rendered.shape[2]
@@ -221,11 +467,8 @@
         .transpose(2, 0, 1, 3)
         .reshape(TILES_DEV, 3, pixel_count)
     )
-    unused, combine_pull = jax.vjp(lambda found: combine(found, tile_ids), results)
-    results_grad = combine_pull(tile_grad)[0]
-    block_grad = run_live(block_pullback, (per_block, results_grad), live, per_block.shape)
-    flat_grad = jnp.moveaxis(block_grad, 0, 1).reshape(9, -1)
-    table_grad = jnp.zeros_like(received).at[:, slot_rows.reshape(-1)].add(flat_grad)
+    tile_grad = jnp.pad(tile_grad, ((0, 0), (0, 5), (0, 0)))
+    table_grad = pull_tiles(tile_ids, info, recs, saved, tile_grad, pairs, received.shape[1])
     back_records = lax.all_to_all(table_grad, "gauss", split_axis=1, concat_axis=1, tiled=True)
     own_grad = jnp.zeros_like(own_records).at[:, send_list].set(back_records)
     unused_colour, shade_pull = jax.vjp(shade, splats[6:9], sh_coeffs)

time: 367 us -> 160 us (0.44)
  blocking collectives: 117 us -> 40.7 us
  other arithmetic: 96.1 us -> 41.2 us
  matrix products: 51.1 us -> 0 us
  loops' own time: 38.3 us -> 0 us
  local copies, waits for them, and re-layouts: 37.7 us -> 15.7 us
  starting transfers between devices: 13.6 us -> 35.2 us
  Pallas kernels: 0 us -> 20.3 us
  waiting for transfers between devices: 9.67 us -> 4.87 us
    all_to_all x1, blocking collectives: 117 us -> 40.7 us  [body(): lax.all_to_all(table_grad, 'gauss', split_axis=1, concat_axis=1, tiled=True)]
    dot_general x148 -> x0, matrix products: 51.1 us -> none  [the longest x72 30.9 us: composite(): jnp.dot(earlier_mask, logged, precision=HIGHEST, preferred_element_type=j...]
    another operation x2 -> x0, loops' own time: 38.3 us -> none  [run_live(): return lax.fori_loop(0, live, advance, jnp.zeros(out_shape, jnp.float32))]
    scatter-add x1 -> x0, other arithmetic: 34.3 us -> none  [body(): jnp.zeros_like(received).at[:, slot_rows.reshape(-1)].add(flat_grad)]
    ppermute x2, starting transfers between devices: 3.65 us -> 25.2 us  [extended(): lax.ppermute(tail, axis, [(i, (i + 1) % count) for i in range(ends)])]
    pallas_call x0 -> x2, Pallas kernels: none -> 20.3 us  [the longest x1 11.5 us: pull_tiles(): pl.pallas_call(backward_kernel, out_shape=jax.ShapeDtypeStruct((9, own),...]
    gather x1 -> x0, local copies, waits for them, and re-layouts: 17.1 us -> none  [body(): received[:, slot_rows.reshape(-1)]]
    reduce_sum x48 -> x1, other arithmetic: 14.3 us -> 0.69 us  [body(): live = jnp.sum((tile_ids < TILES_DEV).astype(jnp.int32))]
  transfers between devices with their start and end apart: 5 -> 5, of which waited for: 4 -> 4; matrix products, arithmetic and copies ran while one was open for 1% -> 3% of each run, Pallas kernels for 0% -> 0%
where the time goes in v1:
time: 160 us; the launch traced here: 159 us
  other arithmetic  41.2 us (26%)
  blocking collectives  40.7 us (25%)
  starting transfers between devices  35.2 us (22%)
  Pallas kernels  20.3 us (13%)
  local copies, waits for them, and re-layouts  15.7 us (10%)
  waiting for transfers between devices  4.87 us (3%)
    all_to_all x1, blocking collectives, body(): lax.all_to_all(table_grad, 'gauss', split_axis=1, concat_axis=1, tiled=True)  40.7 us
    ppermute x2, starting transfers between devices, extended(): lax.ppermute(tail, axis, [(i, (i + 1) % count) for i in range(ends)])  25.2 us
    add x2, other arithmetic, blur(): across = across + weights[offset] * padded[..., :, offset:offset + cols_out]  16 us
    add x2, other arithmetic, blur(): result = result + weights[offset] * across[..., offset:offset + rows_out, :]  14.7 us
    pallas_call x1, Pallas kernels, pull_tiles(): pl.pallas_call(backward_kernel, out_shape=jax.ShapeDtypeStruct((9, own),...  11.5 us
    pallas_call x1, Pallas kernels, draw_tiles(): pl.pallas_call(forward_kernel, out_shape=(jax.ShapeDtypeStruct((TILES_DEV...  8.86 us
    all_to_all x1, starting transfers between devices, body(): lax.all_to_all(own_records[:, send_list], 'gauss', split_axis=1, concat_a...  7.39 us
    scatter x1, local copies, waits for them, and re-layouts, body(): own_grad = jnp.zeros_like(own_records).at[:, send_list].set(back_records)  3.21 us
  transfers between devices with their start and end apart: 5, of which 4 were waited for; matrix products, arithmetic and copies ran while one was open for 3% of the time, Pallas kernels for 0%

profile of v1, /device:TPU:0, one launch (start us, length us, event | category | flops | bytes accessed | tf_op | source)
XLA Modules:
  0.0 159.0 jit_solution(7157518780540702521)
XLA Ops:
  0.7 0.9 multiply_multiply_fusion.1
  1.5 0.8 slice.278
  2.3 0.9 multiply_multiply_fusion.2
  3.3 1.0 multiply_reduce_fusion.1
  4.3 0.2 copy.65
  4.5 0.7 compare_select_fusion
  5.2 2.8 %gather_fusion = f32[1024,9]{1,0:T(8,128)S(1)} fusion(f32[9,1024]{0,1:T(8,128)S(1)} %copy.65, s32[1024]{0:T(1024)S(1)} %get-tuple-element.50), kind=kCustom, calls=%fused_computation | custom fusion | bytes 77824 | tf_op jit(solution)/shard_map/gather | solution.py:435
  8.0 0.2 copy.66
  8.3 0.7 reshape.115
  9.0 7.4 %all-to-all-start = ((f32[16,1,576]{2,1,0:T(1,128)}), f32[16,1,576]{2,1,0:T(1,128)S(1)}, u32[]{:S(2)}, u32[]{:S(2)}) async-start(f32[16,1,576]{2,1,0:T(1,128)} %reshape.115), calls=%async_computation | async-start | bytes 81920 | tf_op jit(solution)/shard_map/all_to_all | solution.py:434
  16.4 0.7 fusion.62
  17.1 0.7 fusion.61
  17.9 0.2 copy.69
  18.1 0.8 reshape.89.slots_ref
  19.0 1.2 pad_add_fusion.1.info_ref
  20.3 2.8 %all-to-all-done = f32[16,1,576]{2,1,0:T(1,128)S(1)} async-done(((f32[16,1,576]{2,1,0:T(1,128)}), f32[16,1,576]{2,1,0:T(1,128)S(1)}, u32[]{:S(2)}, u32[]{:S(2)}) %all-to-all-start) | async-done | bytes 36896 | tf_op jit(solution)/shard_map/all_to_all | solution.py:434
  23.1 0.6 broadcast.401
  23.7 0.7 reduce
  24.5 0.7 all_to_all.17.recv_ref
  25.2 8.9 %draw_tiles.1 = (f32[8,8,256]{2,1,0:T(8,128)}, f32[48,16,128]{2,1,0:T(8,128)}, f32[48,5,8,256]{3,2,1,0:T(8,128)}) custom-call(s32[48]{0:T(128)} %bitcast.98, s32[3]{0:T(128)} %pad_add_fusion.1.info_ref, f32[9,1024]{1,0:T(8,128)} %all_to_all.17.recv_ref, s32[24,256]{1,0:T(8,128)} %reshape.89.slots_ref), custom_call_target="tpu_custom_call" | custom-call | tf_op jit(solution)/shard_map/draw_tiles/pallas_call | solution.py:341
  34.1 0.8 slice.282
  35.3 1.3 collective-permute-start.1
  36.6 4.4 %collective-permute-start = (f32[2,3,10,128]{3,2,1,0:T(8,128)S(1)}, f32[2,3,10,128]{3,2,1,0:T(8,128)S(1)}, u32[]{:S(2)}, u32[]{:S(2)}) collective-permute-start(f32[2,3,10,128]{3,2,1,0:T(8,128)S(1)} %get-tuple-element.45), channel_id=1, source_target_pairs={{0,2},{2,4},{4,6},{6,8},{8,10},{10,12},{12,14},{14,16},{16,18},{18... | collective-permute-start | bytes 92168 | tf_op jit(solution)/shard_map/ppermute | solution.py:43
  40.9 0.6 broadcast_divide_fusion
  41.6 0.2 collective-permute-done
  41.9 1.3 collective-permute-start.3
  43.2 20.8 %collective-permute-start.2 = (f32[2,3,36,10]{3,2,1,0:T(8,128)S(1)}, f32[2,3,36,10]{3,2,1,0:T(8,128)S(1)}, u32[]{:S(2)}, u32[]{:S(2)}) collective-permute-start(f32[2,3,36,10]{3,2,1,0:T(8,128)S(1)} %get-tuple-element.27), channel_id=1, source_target_pairs={{0,1},{2,3},{4,5},{6,7},{8,9},{10,11},{12,13},{14,15},{16,17},{18,... | collective-permute-start | bytes 25928 | tf_op jit(solution)/shard_map/ppermute | solution.py:43
  64.1 0.7 fusion.65
  65.0 1.7 %collective-permute-done.2 = f32[2,3,36,10]{3,2,1,0:T(8,128)S(1)} collective-permute-done((f32[2,3,36,10]{3,2,1,0:T(8,128)S(1)}, f32[2,3,36,10]{3,2,1,0:T(8,128)S(1)}, u32[]{:S(2)}, u32[]{:S(2)}) %collective-permute-start.2) | collective-permute-done | bytes 8672 | tf_op jit(solution)/shard_map/ppermute | solution.py:43
  66.7 0.2 pad_maximum_fusion.1
  66.9 0.2 pad_maximum_fusion
  67.1 8.6 %fusion = f32[5,3,36,138]{3,2,1,0:T(8,128)S(1)} fusion(f32[5,3,36,148]{3,2,1,0:T(8,128)S(1)} %pad_maximum_fusion, f32[]{:T(128)} %bitcast.21, f32[]{:T(128)} %bitcast.20, f32[]{:T(128)} %bitcast.19, f32[]{:T(128)} %bitcast.18, f32[]{:T(128)} %bitcast.17, f32[]{:T(128)} %bitcast.16, f32[]{:T(128)} %bitcast.15, f32[]{:T(128)} %bitcast.14, f32[]{:T(128)} %bitcast.13, ...), kind=kLoop, calls=%fused_computation.3 | loop fusion | flops 1564920 | bytes 3577004 | tf_op jit(solution)/shard_map/add | solution.py:396
  75.7 7.6 %fusion.10 = f32[5,3,26,138]{3,2,1,0:T(8,128)S(1)} fusion(f32[5,3,36,138]{3,2,1,0:T(8,128)S(1)} %fusion, f32[]{:T(128)} %bitcast.21, f32[]{:T(128)} %bitcast.20, f32[]{:T(128)} %bitcast.19, f32[]{:T(128)} %bitcast.18, f32[]{:T(128)} %bitcast.17, f32[]{:T(128)} %bitcast.16, f32[]{:T(128)} %bitcast.15, f32[]{:T(128)} %bitcast.14, f32[]{:T(128)} %bitcast.13, ...), kind=kLoop, calls=%fused_computation.25 | loop fusion | flops 1130220 | bytes 2583404 | tf_op jit(solution)/shard_map/add | solution.py:399
  83.3 0.1 fusion.32
  83.6 7.4 %fusion.22 = f32[3,3,26,128]{3,2,1,0:T(8,128)S(1)} fusion(f32[3,3,26,138]{3,2,1,0:T(8,128)S(1)} %maximum_multiply_fusion, f32[]{:T(128)} %bitcast.21, f32[]{:T(128)} %bitcast.20, f32[]{:T(128)} %bitcast.19, f32[]{:T(128)} %bitcast.18, f32[]{:T(128)} %bitcast.17, f32[]{:T(128)} %bitcast.16, f32[]{:T(128)} %bitcast.15, f32[]{:T(128)} %bitcast.14, f32[]{:T(128)} %bitcast.13, ...), kind=kLoop, calls=%fused_computation.54 | loop fusion | flops 628992 | bytes 1437740 | tf_op jit(solution)/shard_map/add | solution.py:396
  91.0 7.1 %fusion.38 = f32[3,3,16,128]{3,2,1,0:T(8,128)S(1)} fusion(f32[3,3,26,128]{3,2,1,0:T(8,128)S(1)} %fusion.22, f32[]{:T(128)} %bitcast.21, f32[]{:T(128)} %bitcast.20, f32[]{:T(128)} %bitcast.19, f32[]{:T(128)} %bitcast.18, f32[]{:T(128)} %bitcast.17, f32[]{:T(128)} %bitcast.16, f32[]{:T(128)} %bitcast.15, f32[]{:T(128)} %bitcast.14, f32[]{:T(128)} %bitcast.13, ...), kind=kLoop, calls=%fused_computation.95 | loop fusion | flops 387072 | bytes 884780 | tf_op jit(solution)/shard_map/add | solution.py:399
  98.4 0.6 pad.13.grad_ref
  99.1 11.5 %pull_tiles.1 = f32[9,1024]{1,0:T(8,128)} custom-call(s32[48]{0:T(128)} %bitcast.99, s32[3]{0:T(128)} %pad_add_fusion.1.info_ref, f32[48,16,128]{2,1,0:T(8,128)} %get-tuple-element.7.rec_ref, f32[48,5,8,256]{3,2,1,0:T(8,128)} %get-tuple-element.8.saved_ref, f32[8,8,256]{2,1,0:T(8,128)} %pad.13.grad_ref, s32[24,256]{1,0:T(8,128)} %reshape.89.slots_ref), custom_call_target="tpu_custom_call" | custom-call | tf_op jit(solution)/shard_map/pull_tiles/pallas_call | solution.py:362
  110.6 1.0 all_to_all.18
  111.7 40.7 %all_to_all.23 = f32[16,1,576]{2,1,0:T(1,128)S(1)} all-to-all(f32[16,1,576]{2,1,0:T(1,128)S(1)} %reshape.117), channel_id=1, replica_groups=mesh['gauss'=16,'tile'=2] {'gauss'}, dimensions={0} | all-to-all | bytes 73728 | tf_op jit(solution)/shard_map/all_to_all | solution.py:472
  152.4 0.7 reduce.1
  153.3 0.2 copy.77
  153.5 3.2 %scatter_custom_fusion = f32[9,1024]{0,1:T(8,128)S(1)} fusion(s32[1024]{0:T(1024)S(1)} %get-tuple-element.49, f32[1024,9]{1,0:T(8,128)S(1)} %copy.77, f32[]{:T(128)} %constant.23.clone.1), kind=kCustom, calls=%fused_computation.46 | custom fusion | bytes 36868 | tf_op jit(solution)/shard_map/scatter | solution.py:473
  156.8 0.2 slice.415
  157.0 0.2 copy.78
  157.1 0.7 broadcast_multiply_fusion
  158.1 0.2 copy.79
  158.4 0.6 pad_maximum_fusion.4
  (49 shorter events, 2.1 us)
Async XLA Ops:
  0.6 16.4 %copy-start.5 = (s32[1,48]{1,0:T(1,128)S(1)}, s32[1,48]{1,0:T(1,128)}, u32[]{:S(2)}) copy-start(s32[1,48]{1,0:T(1,128)} %param.10) | copy-start | bytes 580
  0.6 17.1 %copy-start.4 = (s32[1,48,128]{2,1,0:T(8,128)S(1)}, s32[1,48,128]{2,1,0:T(8,128)}, u32[]{:S(2)}) copy-start(s32[1,48,128]{2,1,0:T(8,128)} %param.9) | copy-start | bytes 73732
  5.2 30.0 %copy-start.1 = (f32[3,16,128]{2,1,0:T(8,128)S(1)}, f32[3,16,128]{2,1,0:T(8,128)}, u32[]{:S(2)}) copy-start(f32[3,16,128]{2,1,0:T(8,128)} %param.11) | copy-start | bytes 73732
  9.0 14.1 %all-to-all-start = ((f32[16,1,576]{2,1,0:T(1,128)}), f32[16,1,576]{2,1,0:T(1,128)S(1)}, u32[]{:S(2)}, u32[]{:S(2)}) async-start(f32[16,1,576]{2,1,0:T(1,128)} %reshape.115), calls=%async_computation | async-start | bytes 81920 | tf_op jit(solution)/shard_map/all_to_all | solution.py:434
  35.3 6.3 %collective-permute-start.1 = (f32[2,3,10,128]{3,2,1,0:T(8,128)S(1)}, f32[2,3,10,128]{3,2,1,0:T(8,128)S(1)}, u32[]{:S(2)}, u32[]{:S(2)}) collective-permute-start(f32[2,3,10,128]{3,2,1,0:T(8,128)S(1)} %get-tuple-element.46), channel_id=1, source_target_pairs={{2,0},{4,2},{6,4},{8,6},{10,8},{12,10},{14,12},{16,14},{18,16},{20... | collective-permute-start | bytes 92168 | tf_op jit(solution)/shard_map/ppermute | solution.py:45
  36.6 5.2 %collective-permute-start = (f32[2,3,10,128]{3,2,1,0:T(8,128)S(1)}, f32[2,3,10,128]{3,2,1,0:T(8,128)S(1)}, u32[]{:S(2)}, u32[]{:S(2)}) collective-permute-start(f32[2,3,10,128]{3,2,1,0:T(8,128)S(1)} %get-tuple-element.45), channel_id=1, source_target_pairs={{0,2},{2,4},{4,6},{6,8},{8,10},{10,12},{12,14},{14,16},{16,18},{18... | collective-permute-start | bytes 92168 | tf_op jit(solution)/shard_map/ppermute | solution.py:43
  41.9 23.1 %collective-permute-start.3 = (f32[2,3,36,10]{3,2,1,0:T(8,128)S(1)}, f32[2,3,36,10]{3,2,1,0:T(8,128)S(1)}, u32[]{:S(2)}, u32[]{:S(2)}) collective-permute-start(f32[2,3,36,10]{3,2,1,0:T(8,128)S(1)} %get-tuple-element.28), channel_id=1, source_target_pairs={{1,0},{3,2},{5,4},{7,6},{9,8},{11,10},{13,12},{15,14},{17,16},{19,... | collective-permute-start | bytes 25928 | tf_op jit(solution)/shard_map/ppermute | solution.py:45
  43.2 23.5 %collective-permute-start.2 = (f32[2,3,36,10]{3,2,1,0:T(8,128)S(1)}, f32[2,3,36,10]{3,2,1,0:T(8,128)S(1)}, u32[]{:S(2)}, u32[]{:S(2)}) collective-permute-start(f32[2,3,36,10]{3,2,1,0:T(8,128)S(1)} %get-tuple-element.27), channel_id=1, source_target_pairs={{0,1},{2,3},{4,5},{6,7},{8,9},{10,11},{12,13},{14,15},{16,17},{18,... | collective-permute-start | bytes 25928 | tf_op jit(solution)/shard_map/ppermute | solution.py:43
  64.9 33.2 %copy-start.3 = (f32[3,16,128]{2,1,0:T(8,128)}, f32[3,16,128]{2,1,0:T(8,128)S(1)}, u32[]{:S(2)}) copy-start(f32[3,16,128]{2,1,0:T(8,128)S(1)} %reshape.91) | copy-start | bytes 73732
  110.6 46.6 %copy-start = (f32[48,1024]{1,0:T(8,128)S(1)}, f32[48,1024]{1,0:T(8,128)}, u32[]{:S(2)}) copy-start(f32[48,1024]{1,0:T(8,128)} %param.7) | copy-start | bytes 589828
  111.7 46.2 %copy-start.2 = (f32[9,1024]{1,0:T(8,128)S(1)}, f32[9,1024]{1,0:T(8,128)}, u32[]{:S(2)}) copy-start(f32[9,1024]{1,0:T(8,128)} %param.6) | copy-start | bytes 110596

commit v2 on v1

--- a/solution.py
+++ b/solution.py
@@ -1,3 +1,6 @@
+import functools
+import math
+
 import jax
 import jax.numpy as jnp
 from jax import lax
@@ -30,23 +33,6 @@
 )
 CONST_ONE = 0.0001
 CONST_TWO = 0.0009
-
-
-def extended(cells, sides, width):
-    for axis, dim in sides:
-        count = lax.axis_size(axis)
-        ends = count - 1
-        head = lax.slice_in_dim(cells, 0, width, axis=dim)
-        tail = lax.slice_in_dim(cells, cells.shape[dim] - width, cells.shape[dim], axis=dim)
-        cells = jnp.concatenate(
-            [
-                lax.ppermute(tail, axis, [(i, (i + 1) % count) for i in range(ends)]),
-                cells,
-                lax.ppermute(head, axis, [((i + 1) % count, i) for i in range(ends)]),
-            ],
-            axis=dim,
-        )
-    return cells
 
 
 def harmonics(direction):
@@ -117,7 +103,8 @@
 
 
 def forward_kernel(
-    tile_ref, info_ref, recv_ref, slots_ref, image_ref, rec_ref, saved_ref, pad_ref, split_ref, col_ref
+    tile_ref, info_ref, recv_ref, slots_ref, picture_ref, rec_ref, saved_ref,
+    pad_ref, split_ref, col_ref, image_ref,
 ):
     live = info_ref[0]
     own = recv_ref.shape[1]
@@ -196,6 +183,20 @@
 
     ones = jnp.ones((1, HALF), jnp.float32)
     lax.fori_loop(0, live, draw, (ones, ones))
+    lane_tile = lax.broadcasted_iota(jnp.int32, (SEGMENTS, HALF), 1) // TILE_SIDE
+    for side in range(2):
+        lanes = slice(side * HALF, (side + 1) * HALF)
+        for c in range(3):
+            shown = jnp.zeros((SEGMENTS, HALF), jnp.float32)
+            for tile in range(TILES_DEV):
+                row = jnp.broadcast_to(image_ref[tile, c : c + 1, lanes], (SEGMENTS, HALF))
+                moved = pltpu.roll(row, TILE_SIDE * tile, 1) if tile else row
+                for bit in (1, 2, 4):
+                    moved = jnp.where(
+                        (seg_at & bit) > 0, pltpu.roll(moved, HALF - TILE_SIDE * bit, 1), moved
+                    )
+                shown = jnp.where(lane_tile == tile, moved, shown)
+            picture_ref[c, side * SEGMENTS : (side + 1) * SEGMENTS, :] = shown
 
 
 def backward_kernel(
@@ -341,7 +342,7 @@
     return pl.pallas_call(
         forward_kernel,
         out_shape=(
-            jax.ShapeDtypeStruct((TILES_DEV, 8, side), jnp.float32),
+            jax.ShapeDtypeStruct((3, TILE_SIDE, TILES_DEV * TILE_SIDE), jnp.float32),
             jax.ShapeDtypeStruct((slots_total, 16, BLOCK), jnp.float32),
             jax.ShapeDtypeStruct((slots_total, 5, SEGMENTS, side), jnp.float32),
         ),
@@ -351,6 +352,7 @@
             pltpu.VMEM((16, own), jnp.float32),
             pltpu.VMEM((48, own), jnp.bfloat16),
             pltpu.VMEM((BLOCK, 16), jnp.float32),
+            pltpu.VMEM((TILES_DEV, 8, side), jnp.float32),
         ],
         name="draw_tiles",
     )(tile_ids, info, received, pairs)
@@ -375,54 +377,184 @@
     )(tile_ids, info, recs, saved, grads, pairs)
 
 
-def to_image(tiles_img):
-    return (
-        tiles_img.reshape(TILES_DEV, 3, TILE_SIDE, TILE_SIDE)
-        .transpose(1, 2, 0, 3)
-        .reshape(3, TILE_SIDE, TILES_DEV * TILE_SIDE)
+WAYS = [(down, right) for down in (-1, 0, 1) for right in (-1, 0, 1) if (down, right) != (0, 0)]
+NORM = sum(math.exp(-m * m / 4.5) for m in range(-5, 6))
+
+
+def halo_kernel(bands, cols_total, shown_ref, target_ref, out_ref, send_sem, recv_sem):
+    band = lax.axis_index("gauss")
+    column = lax.axis_index("tile")
+    rows, cols = shown_ref.shape[1:]
+    out_ref[...] = jnp.zeros_like(out_ref)
+    barrier = pltpu.get_barrier_semaphore()
+
+    def exists(way):
+        there_band = band + way[0]
+        there_col = column + way[1]
+        return (
+            (there_band >= 0) & (there_band < bands) & (there_col >= 0) & (there_col < cols_total)
+        )
+
+    def copies(at):
+        down, right = WAYS[at]
+        landing = len(WAYS) - 1 - at
+        return [
+            pltpu.make_async_remote_copy(
+                src_ref=source,
+                dst_ref=out_ref.at[
+                    pl.ds(3 * kind, 3), pl.ds(rows * (1 - down), rows), pl.ds(cols * (1 - right), cols)
+                ],
+                send_sem=send_sem.at[kind, at],
+                recv_sem=recv_sem.at[kind, landing],
+                device_id=(band + down, column + right),
+                device_id_type=pl.DeviceIdType.MESH,
+            )
+            for kind, source in enumerate((shown_ref, target_ref))
+        ]
+
+    for at, way in enumerate(WAYS):
+
+        @pl.when(exists(way))
+        def _(way=way):
+            pl.semaphore_signal(
+                barrier,
+                inc=1,
+                device_id=(band + way[0], column + way[1]),
+                device_id_type=pl.DeviceIdType.MESH,
+            )
+
+    peers = sum(exists(way).astype(jnp.int32) for way in WAYS)
+    pl.semaphore_wait(barrier, peers)
+
+    for at, way in enumerate(WAYS):
+
+        @pl.when(exists(way))
+        def _(at=at):
+            for copy in copies(at):
+                copy.start()
+
+    out_ref[0:3, rows : 2 * rows, cols : 2 * cols] = shown_ref[...]
+    out_ref[3:6, rows : 2 * rows, cols : 2 * cols] = target_ref[...]
+    for at, way in enumerate(WAYS):
+
+        @pl.when(exists(way))
+        def _(at=at):
+            for copy in copies(at):
+                copy.wait_send()
+            for kind, source in enumerate((shown_ref, target_ref)):
+                pltpu.make_async_remote_copy(
+                    src_ref=source,
+                    dst_ref=out_ref.at[
+                        pl.ds(3 * kind, 3),
+                        pl.ds(rows * (1 + WAYS[at][0]), rows),
+                        pl.ds(cols * (1 + WAYS[at][1]), cols),
+                    ],
+                    send_sem=send_sem.at[kind, at],
+                    recv_sem=recv_sem.at[kind, at],
+                    device_id=(band + WAYS[at][0], column + WAYS[at][1]),
+                    device_id_type=pl.DeviceIdType.MESH,
+                ).wait_recv()
+
+
+def exchange(rendered, target):
+    channels, rows, cols = rendered.shape
+    return pl.pallas_call(
+        functools.partial(halo_kernel, lax.axis_size("gauss"), lax.axis_size("tile")),
+        out_shape=jax.ShapeDtypeStruct((2 * channels, 3 * rows, 3 * cols), jnp.float32),
+        in_specs=[vmem(), vmem()],
+        out_specs=vmem(),
+        scratch_shapes=[
+            pltpu.SemaphoreType.DMA((2, len(WAYS))),
+            pltpu.SemaphoreType.DMA((2, len(WAYS))),
+        ],
+        compiler_params=pltpu.CompilerParams(collective_id=0, has_side_effects=True),
+        name="halo",
+    )(rendered, target)
+
+
+def banded(shape, offset):
+    gap = (
+        lax.broadcasted_iota(jnp.int32, shape, 0) - lax.broadcasted_iota(jnp.int32, shape, 1) + offset
+    ).astype(jnp.float32)
+    return jnp.where(jnp.abs(gap) < 5.5, jnp.exp(gap * gap / -4.5) * (1.0 / NORM), 0.0)
+
+
+def exact_dot(left, right):
+    return jnp.dot(left, right, precision=HIGHEST, preferred_element_type=jnp.float32)
+
+
+def ssim_kernel(place_ref, wide_ref, out_ref, stack_ref):
+    tall, wide = wide_ref.shape[1:]
+    rows, cols = tall // 3, wide // 3
+    row_from, rows_mid = rows // 2, 2 * rows
+    col_from, cols_mid = cols // 2, 2 * cols
+    for c in range(3):
+        pic = wide_ref[c]
+        aim = wide_ref[3 + c]
+        for kind, plane in enumerate((pic, aim, pic * pic + aim * aim, pic * aim)):
+            at = 3 * kind + c
+            stack_ref[at * tall : (at + 1) * tall, :] = plane
+    across = exact_dot(stack_ref[...], banded((wide, cols_mid), -col_from))
+    moments = exact_dot(
+        banded((rows_mid, tall), row_from),
+        jnp.concatenate([across[at * tall : (at + 1) * tall] for at in range(12)], axis=1),
     )
-
-
-def window():
-    tap_offsets = jnp.arange(11).astype(jnp.float32) - 5.0
-    profile = jnp.exp(-tap_offsets * tap_offsets / 4.5)
-    return profile / jnp.sum(profile)
-
-
-def blur(padded, rows_out, cols_out):
-    weights = window()
-    across = weights[0] * padded[..., :, 0:cols_out]
-    for offset in range(1, 11):
-        across = across + weights[offset] * padded[..., :, offset : offset + cols_out]
-    result = weights[0] * across[..., 0:rows_out, :]
-    for offset in range(1, 11):
-        result = result + weights[offset] * across[..., offset : offset + rows_out, :]
-    return result
-
-
-def similarity(mu_x, mu_y, sq_x, sq_y, cross_xy):
-    mean_xy = mu_x * mu_y
-    numerator = (2.0 * mean_xy + CONST_ONE) * (2.0 * (cross_xy - mean_xy) + CONST_TWO)
-    denominator = (mu_x * mu_x + mu_y * mu_y + CONST_ONE) * (
-        sq_x - mu_x * mu_x + sq_y - mu_y * mu_y + CONST_TWO
+    row_at = place_ref[0] + row_from - rows + lax.broadcasted_iota(jnp.int32, (rows_mid, cols_mid), 0)
+    col_at = place_ref[1] + col_from - cols + lax.broadcasted_iota(jnp.int32, (rows_mid, cols_mid), 1)
+    inside = (row_at >= 0) & (row_at < place_ref[2]) & (col_at >= 0) & (col_at < place_ref[3])
+    slopes = [None] * 9
+    for c in range(3):
+        mu_x, mu_y, squares, cross = [
+            moments[:, (3 * kind + c) * cols_mid : (3 * kind + c + 1) * cols_mid] for kind in range(4)
+        ]
+        mean_xy = mu_x * mu_y
+        mean_sq = mu_x * mu_x + mu_y * mu_y
+        top_1 = 2.0 * mean_xy + CONST_ONE
+        top_2 = 2.0 * (cross - mean_xy) + CONST_TWO
+        low_1 = mean_sq + CONST_ONE
+        low_2 = squares - mean_sq + CONST_TWO
+        inverse = -0.2 / (low_1 * low_2)
+        value = top_1 * top_2 * inverse
+        value_1 = value * low_2 * inverse * -5.0
+        value_2 = value * low_1 * inverse * -5.0
+        slope_mean = 2.0 * mu_y * (top_2 - top_1) * inverse - 2.0 * mu_x * (value_1 - value_2)
+        for kind, slope in enumerate((slope_mean, -value_2, 2.0 * top_1 * inverse)):
+            slopes[3 * kind + c] = jnp.where(inside, slope, 0.0)
+    down = exact_dot(
+        banded((rows, rows_mid), rows - row_from), jnp.concatenate(slopes, axis=1)
     )
-    return numerator / denominator
-
-
-def five_products(padded):
-    return jnp.stack(
-        [padded[0], padded[1], padded[0] * padded[0], padded[1] * padded[1], padded[0] * padded[1]]
+    spread = exact_dot(
+        jnp.concatenate([down[:, at * cols_mid : (at + 1) * cols_mid] for at in range(9)], axis=0),
+        banded((cols_mid, cols), col_from - cols),
     )
-
-
-def similarity_grads(moments):
-
-    def partial_loss(mean_x, square_x, product_xy):
-        return jnp.sum(
-            0.2 * (1.0 - similarity(mean_x, moments[1], square_x, moments[3], product_xy))
-        )
-
-    return jnp.stack(jax.grad(partial_loss, argnums=(0, 1, 2))(moments[0], moments[2], moments[4]))
+    lane_row = lax.broadcasted_iota(jnp.int32, (SEGMENTS, HALF), 1) // TILE_SIDE
+    seg_at = lax.broadcasted_iota(jnp.int32, (SEGMENTS, HALF), 0)
+    out_ref[...] = jnp.zeros_like(out_ref)
+    for c in range(3):
+        pic = wide_ref[c, rows : 2 * rows, cols : 2 * cols]
+        aim = wide_ref[3 + c, rows : 2 * rows, cols : 2 * cols]
+        parts = [spread[(3 * kind + c) * rows : (3 * kind + c + 1) * rows] for kind in range(3)]
+        total = parts[0] + 2.0 * pic * parts[1] + aim * parts[2] + 1.6 * (pic - aim)
+        for side in range(2):
+            part = total[side * SEGMENTS : (side + 1) * SEGMENTS]
+            skewed = pltpu.roll(part, 0, 1, stride=TILE_SIDE, stride_axis=0)
+            for tile in range(TILES_DEV):
+                moved = pltpu.roll(skewed, HALF - TILE_SIDE * tile, 1) if tile else skewed
+                kept = jnp.where(lane_row == seg_at, moved, 0.0)
+                out_ref[tile, c : c + 1, side * HALF : (side + 1) * HALF] = jnp.sum(
+                    kept, axis=0, keepdims=True
+                )
+
+
+def ssim_pull(place, wide):
+    return pl.pallas_call(
+        ssim_kernel,
+        out_shape=jax.ShapeDtypeStruct((TILES_DEV, 8, TILE_SIDE * TILE_SIDE), jnp.float32),
+        in_specs=[smem(), vmem()],
+        out_specs=vmem(),
+        scratch_shapes=[pltpu.VMEM((12 * wide.shape[1], wide.shape[2]), jnp.float32)],
+        name="ssim_pull",
+    )(place, wide)
 
 
 def body(splats, sh_coeffs, send_list, block_slots, block_tiles, target):
@@ -438,36 +570,18 @@
     slot_rows = block_slots[0]
     slots_total = slot_rows.shape[0]
     live = jnp.sum((tile_ids < TILES_DEV).astype(jnp.int32))
-    pixel_count = TILE_SIDE * TILE_SIDE
     info = jnp.stack([live, TILE_SIDE * TILES_DEV * col_band, TILE_SIDE * row_band]).astype(jnp.int32)
     pairs = (
         slot_rows.reshape(slots_total, SEGMENTS, STEPS)
         .transpose(0, 2, 1)
         .reshape(slots_total // 2, 2 * BLOCK)
     )
-    tiles_img, recs, saved = draw_tiles(tile_ids, info, received, pairs, slots_total)
-    tiles_img = tiles_img[:, 0:3]
-    rendered = to_image(tiles_img)
-    rows_here = rendered.shape[1]
-    cols_here = rendered.shape[2]
-    padded = extended(jnp.stack([rendered, target]), (("gauss", 2), ("tile", 3)), 10)
-    moments = blur(five_products(padded), rows_here + 10, cols_here + 10)
-    grads_map = similarity_grads(moments)
-    row_ids = row_band * rows_here - 5 + jnp.arange(rows_here + 10)
-    col_ids = col_band * cols_here - 5 + jnp.arange(cols_here + 10)
-    inside = ((row_ids >= 0) & (row_ids < rows_here * owners))[:, None] & (
-        (col_ids >= 0) & (col_ids < cols_here * peers)
-    )[None, :]
-    spread = blur(grads_map * inside.astype(jnp.float32), rows_here, cols_here)
-    pixel_grad = (
-        spread[0] + 2.0 * rendered * spread[1] + target * spread[2] + 1.6 * (rendered - target)
-    )
-    tile_grad = (
-        pixel_grad.reshape(3, TILE_SIDE, TILES_DEV, TILE_SIDE)
-        .transpose(2, 0, 1, 3)
-        .reshape(TILES_DEV, 3, pixel_count)
-    )
-    tile_grad = jnp.pad(tile_grad, ((0, 0), (0, 5), (0, 0)))
+    rendered, recs, saved = draw_tiles(tile_ids, info, received, pairs, slots_total)
+    rows_here, cols_here = rendered.shape[1:]
+    place = jnp.stack(
+        [row_band * rows_here, col_band * cols_here, rows_here * owners, cols_here * peers]
+    ).astype(jnp.int32)
+    tile_grad = ssim_pull(place, exchange(rendered, target))
     table_grad = pull_tiles(tile_ids, info, recs, saved, tile_grad, pairs, received.shape[1])
     back_records = lax.all_to_all(table_grad, "gauss", split_axis=1, concat_axis=1, tiled=True)
     own_grad = jnp.zeros_like(own_records).at[:, send_list].set(back_records)

time: 160 us -> 122 us (0.76)
  Pallas kernels: 20.3 us -> 53 us
  other arithmetic: 41.2 us -> 8.92 us
  starting transfers between devices: 35.2 us -> 7.38 us
  blocking collectives: 40.7 us -> 34 us
  local copies, waits for them, and re-layouts: 15.7 us -> 12.7 us
  waiting for transfers between devices: 4.87 us -> 2.92 us
    add x5 -> x0, other arithmetic: 30.7 us -> none  [the longest x2 16 us: blur(): across = across + weights[offset] * padded[..., :, offset:offset + cols_out]]
    pallas_call x1 -> x3, Pallas kernels: 8.86 us -> 39.1 us  [the longest x1 23.6 us: exchange(): pl.pallas_call(functools.partial(halo_kernel, lax.axis_size('gauss'), lax...]
    ppermute x4 -> x0, starting transfers between devices: 27.8 us -> none  [the longest x2 25.2 us: extended(): lax.ppermute(tail, axis, [(i, (i + 1) % count) for i in range(ends)])]
    all_to_all x1, blocking collectives: 40.7 us -> 34 us  [body(): lax.all_to_all(table_grad, 'gauss', split_axis=1, concat_axis=1, tiled=True)]
    pallas_call x1, Pallas kernels: 11.5 us -> 13.9 us  [pull_tiles(): pl.pallas_call(backward_kernel, out_shape=jax.ShapeDtypeStruct((9, own),...]
    ppermute x4 -> x0, waiting for transfers between devices: 2.03 us -> none  [the longest x2 1.93 us: extended(): lax.ppermute(tail, axis, [(i, (i + 1) % count) for i in range(ends)])]
    slice x4 -> x0, local copies, waits for them, and re-layouts: 1.62 us -> none  [the longest x2 0.85 us: body(): tiles_img = tiles_img[:, 0:3]]
  transfers between devices with their start and end apart: 5 -> 1, of which waited for: 4 -> 1; matrix products, arithmetic and copies ran while one was open for 3% -> 3% of each run, Pallas kernels for 0% -> 0%
where the time goes in v2:
time: 122 us; the launch traced here: 120 us
  Pallas kernels  53 us (43%)
  blocking collectives  34 us (28%)
  local copies, waits for them, and re-layouts  12.7 us (10%)
  other arithmetic  8.92 us (7%)
  starting transfers between devices  7.38 us (6%)
  waiting for transfers between devices  2.92 us (2%)
    all_to_all x1, blocking collectives, body(): lax.all_to_all(table_grad, 'gauss', split_axis=1, concat_axis=1, tiled=True)  34 us
    pallas_call x1, Pallas kernels, exchange(): pl.pallas_call(functools.partial(halo_kernel, lax.axis_size('gauss'), lax...  23.6 us
    pallas_call x1, Pallas kernels, pull_tiles(): pl.pallas_call(backward_kernel, out_shape=jax.ShapeDtypeStruct((9, own),...  13.9 us
    pallas_call x1, Pallas kernels, draw_tiles(): pl.pallas_call(forward_kernel, out_shape=(jax.ShapeDtypeStruct((3, TILE_S...  10.6 us
    all_to_all x1, starting transfers between devices, body(): lax.all_to_all(own_records[:, send_list], 'gauss', split_axis=1, concat_a...  7.38 us
    pallas_call x1, Pallas kernels, ssim_pull(): pl.pallas_call(ssim_kernel, out_shape=jax.ShapeDtypeStruct((TILES_DEV, 8,...  4.9 us
    scatter x1, local copies, waits for them, and re-layouts, body(): own_grad = jnp.zeros_like(own_records).at[:, send_list].set(back_records)  3.21 us
    all_to_all x1, waiting for transfers between devices, body(): lax.all_to_all(own_records[:, send_list], 'gauss', split_axis=1, concat_a...  2.92 us
  transfers between devices with their start and end apart: 1, of which 1 were waited for; matrix products, arithmetic and copies ran while one was open for 3% of the time, Pallas kernels for 0%

profile of v2, /device:TPU:0, one launch (start us, length us, event | category | flops | bytes accessed | tf_op | source)
XLA Modules:
  0.0 119.7 jit_solution(6238060186988013569)
XLA Ops:
  0.6 0.0 copy-start.3
  0.6 0.0 copy-start.2
  0.7 0.8 slice.28
  1.4 0.9 multiply_multiply_fusion
  2.3 0.7 compare_select_fusion
  3.0 0.9 multiply_multiply_fusion.1
  3.9 0.1 stack.16
  4.0 1.0 multiply_reduce_fusion.1
  5.0 0.2 copy.38
  5.2 2.8 %gather_fusion = f32[1024,9]{1,0:T(8,128)S(1)} fusion(f32[9,1024]{0,1:T(8,128)S(1)} %copy.38, s32[1024]{0:T(1024)S(1)} %get-tuple-element.36), kind=kCustom, calls=%fused_computation | custom fusion | bytes 77824 | tf_op jit(solution)/shard_map/gather | solution.py:567
  8.1 0.2 copy.39
  8.3 0.7 reshape.57
  9.0 7.4 %all-to-all-start = ((f32[16,1,576]{2,1,0:T(1,128)}), f32[16,1,576]{2,1,0:T(1,128)S(1)}, u32[]{:S(2)}, u32[]{:S(2)}) async-start(f32[16,1,576]{2,1,0:T(1,128)} %reshape.57), calls=%async_computation | async-start | bytes 81920 | tf_op jit(solution)/shard_map/all_to_all | solution.py:566
  16.4 0.0 copy-done.3
  16.4 0.7 fusion.8
  17.1 0.0 copy-done.2
  17.1 0.1 copy.41
  17.2 0.2 copy.42
  17.5 0.8 reshape.35.slots_ref
  18.3 1.3 %pad_add_fusion.1.info_ref = s32[3]{0:T(128)} fusion(s32[1]{0:T(128)} %bitcast.3, s32[1]{0:T(128)} %bitcast.2, s32[1]{0:T(128)} %bitcast.1), kind=kLoop, calls=%fused_computation.55 | loop fusion | flops 6 | bytes 24 | tf_op jit(solution)/shard_map/stack | solution.py:573
  19.6 0.6 pad_add_fusion.2.place_ref
  20.2 2.9 %all-to-all-done = f32[16,1,576]{2,1,0:T(1,128)S(1)} async-done(((f32[16,1,576]{2,1,0:T(1,128)}), f32[16,1,576]{2,1,0:T(1,128)S(1)}, u32[]{:S(2)}, u32[]{:S(2)}) %all-to-all-start) | async-done | bytes 36896 | tf_op jit(solution)/shard_map/all_to_all | solution.py:566
  23.1 0.5 broadcast.272
  23.6 0.6 reduce
  24.2 0.1 reshape.58
  24.3 0.7 all_to_all.17.recv_ref
  25.1 10.6 %draw_tiles.1 = (f32[3,16,128]{2,1,0:T(8,128)}, f32[48,16,128]{2,1,0:T(8,128)}, f32[48,5,8,256]{3,2,1,0:T(8,128)}) custom-call(s32[48]{0:T(128)} %bitcast.47, s32[3]{0:T(128)} %pad_add_fusion.1.info_ref, f32[9,1024]{1,0:T(8,128)} %all_to_all.17.recv_ref, s32[24,256]{1,0:T(8,128)} %reshape.35.slots_ref), custom_call_target="tpu_custom_call" | custom-call | tf_op jit(solution)/shard_map/draw_tiles/pallas_call | solution.py:342
  35.6 23.6 %halo.1.wide_ref = f32[6,48,384]{2,1,0:T(8,128)} custom-call(f32[3,16,128]{2,1,0:T(8,128)} %get-tuple-element.12.shown_ref, f32[3,16,128]{2,1,0:T(8,128)} %target_ref.1), custom_call_target="tpu_custom_call" | custom-call | tf_op jit(solution)/shard_map/halo/pallas_call | solution.py:461
  59.2 4.9 %ssim_pull.1.grad_ref = f32[8,8,256]{2,1,0:T(8,128)} custom-call(s32[4]{0:T(128)} %pad_add_fusion.2.place_ref, f32[6,48,384]{2,1,0:T(8,128)} %halo.1.wide_ref), custom_call_target="tpu_custom_call" | custom-call | tf_op jit(solution)/shard_map/ssim_pull/pallas_call | solution.py:550
  64.1 13.9 %pull_tiles.1 = f32[9,1024]{1,0:T(8,128)} custom-call(s32[48]{0:T(128)} %bitcast.48, s32[3]{0:T(128)} %pad_add_fusion.1.info_ref, f32[48,16,128]{2,1,0:T(8,128)} %get-tuple-element.7.rec_ref, f32[48,5,8,256]{3,2,1,0:T(8,128)} %get-tuple-element.8.saved_ref, f32[8,8,256]{2,1,0:T(8,128)} %ssim_pull.1.grad_ref, s32[24,256]{1,0:T(8,128)} %reshape.35.slots_ref), custom_call_target="tpu_custom_call" | custom-call | tf_op jit(solution)/shard_map/pull_tiles/pallas_call | solution.py:364
  78.0 1.0 all_to_all.18
  79.0 0.1 reshape.59
  79.1 0.0 copy-start.1
  79.1 34.0 %all_to_all.23 = f32[16,1,576]{2,1,0:T(1,128)S(1)} all-to-all(f32[16,1,576]{2,1,0:T(1,128)S(1)} %reshape.59), channel_id=1, replica_groups=mesh['gauss'=16,'tile'=2] {'gauss'}, dimensions={0} | all-to-all | bytes 73728 | tf_op jit(solution)/shard_map/all_to_all | solution.py:586
  113.2 0.6 reduce.1
  113.8 0.1 reshape.60
  113.9 0.1 reshape.46
  114.0 0.2 copy.45
  114.2 3.2 %scatter_custom_fusion = f32[9,1024]{0,1:T(8,128)S(1)} fusion(s32[1024]{0:T(1024)S(1)} %get-tuple-element.35, f32[1024,9]{1,0:T(8,128)S(1)} %copy.45, f32[]{:T(128)} %constant.23.clone.1), kind=kCustom, calls=%fused_computation.2 | custom fusion | bytes 36868 | tf_op jit(solution)/shard_map/scatter | solution.py:587
  117.4 0.2 slice.37
  117.6 0.2 copy.46
  117.8 0.0 copy-done
  117.8 0.7 broadcast_multiply_fusion
  118.6 0.1 add_add_fusion
  118.6 0.1 add_add_fusion.1
  118.7 0.1 add_add_fusion.2
  118.8 0.2 copy.47
  119.0 0.6 pad_maximum_fusion.1
  (10 shorter events, 0.1 us)
Async XLA Ops:
  0.6 15.8 %copy-start.3 = (s32[1,48]{1,0:T(1,128)S(1)}, s32[1,48]{1,0:T(1,128)}, u32[]{:S(2)}) copy-start(s32[1,48]{1,0:T(1,128)} %param.10) | copy-start | bytes 580
  0.6 16.5 %copy-start.2 = (s32[1,48,128]{2,1,0:T(8,128)S(1)}, s32[1,48,128]{2,1,0:T(8,128)}, u32[]{:S(2)}) copy-start(s32[1,48,128]{2,1,0:T(8,128)} %param.9) | copy-start | bytes 73732
  9.0 14.1 %all-to-all-start = ((f32[16,1,576]{2,1,0:T(1,128)}), f32[16,1,576]{2,1,0:T(1,128)S(1)}, u32[]{:S(2)}, u32[]{:S(2)}) async-start(f32[16,1,576]{2,1,0:T(1,128)} %reshape.57), calls=%async_computation | async-start | bytes 81920 | tf_op jit(solution)/shard_map/all_to_all | solution.py:566
  78.0 39.8 %copy-start = (f32[48,1024]{1,0:T(8,128)S(1)}, f32[48,1024]{1,0:T(8,128)}, u32[]{:S(2)}) copy-start(f32[48,1024]{1,0:T(8,128)} %param.7) | copy-start | bytes 589828
  79.1 39.4 %copy-start.1 = (f32[9,1024]{1,0:T(8,128)S(1)}, f32[9,1024]{1,0:T(8,128)}, u32[]{:S(2)}) copy-start(f32[9,1024]{1,0:T(8,128)} %param.6) | copy-start | bytes 110596

commit v3 on v2

--- a/solution.py
+++ b/solution.py
@@ -90,9 +90,32 @@
     return along, (down, down + float(HALF // TILE_SIDE))
 
 
+def thirds(value):
+    first = value.astype(jnp.bfloat16)
+    rest = value - first.astype(jnp.float32)
+    second = rest.astype(jnp.bfloat16)
+    third = (rest - second.astype(jnp.float32)).astype(jnp.bfloat16)
+    return first, second, third
+
+
+def fill_widener(wide_ref):
+    rows_at = lax.broadcasted_iota(jnp.int32, wide_ref.shape, 0) % 16
+    field_at = lax.broadcasted_iota(jnp.int32, wide_ref.shape, 1) // HALF
+    wide_ref[...] = jnp.where(rows_at == field_at, 1.0, 0.0).astype(jnp.bfloat16)
+
+
+def widen(rec, wide_ref, column_ref):
+    column_ref[...] = lax.dot_general(
+        jnp.concatenate(thirds(rec), axis=0),
+        wide_ref[...],
+        (((0,), (0,)), ((), ())),
+        preferred_element_type=jnp.float32,
+    )
+
+
 def columns_of(col_ref, step):
-    sub = col_ref[step * SEGMENTS : (step + 1) * SEGMENTS, :]
-    return [jnp.broadcast_to(sub[:, k : k + 1], (SEGMENTS, HALF)) for k in range(9)]
+    rows = slice(step * SEGMENTS, (step + 1) * SEGMENTS)
+    return [col_ref[rows, k * HALF : (k + 1) * HALF] for k in range(9)]
 
 
 def alphas_of(cols, along, down):
@@ -104,20 +127,15 @@
 
 def forward_kernel(
     tile_ref, info_ref, recv_ref, slots_ref, picture_ref, rec_ref, saved_ref,
-    pad_ref, split_ref, col_ref, image_ref,
+    pad_ref, split_ref, col_ref, image_ref, wide_ref,
 ):
     live = info_ref[0]
     own = recv_ref.shape[1]
     pad_ref[...] = jnp.zeros_like(pad_ref)
     pad_ref[0:9, :] = recv_ref[...]
-    whole = pad_ref[...]
-    first = whole.astype(jnp.bfloat16)
-    rest = whole - first.astype(jnp.float32)
-    second = rest.astype(jnp.bfloat16)
-    third = (rest - second.astype(jnp.float32)).astype(jnp.bfloat16)
-    split_ref[0:16, :] = first
-    split_ref[16:32, :] = second
-    split_ref[32:48, :] = third
+    for at, part in enumerate(thirds(pad_ref[...])):
+        split_ref[16 * at : 16 * (at + 1), :] = part
+    fill_widener(wide_ref)
     row_at = lax.broadcasted_iota(jnp.int32, (16, BLOCK), 0)
     base_y = info_ref[2].astype(jnp.float32) + CENTRE
 
@@ -148,19 +166,22 @@
     along, downs = pixel_axes()
     seg_at = lax.broadcasted_iota(jnp.int32, (SEGMENTS, HALF), 0)
 
-    def draw(slot, carry):
-        tile = tile_ref[slot]
-        fresh = (slot == 0) | (tile != tile_ref[jnp.maximum(slot - 1, 0)])
-        col_ref[...] = jnp.transpose(rec_ref[slot])
+    def draw_local(slot, column_ref):
+        widen(rec_ref[slot], wide_ref, column_ref)
         through = [jnp.ones((SEGMENTS, HALF), jnp.float32) for side in range(2)]
         sums = [[jnp.zeros((SEGMENTS, HALF), jnp.float32) for c in range(3)] for side in range(2)]
         for step in range(STEPS):
-            cols = columns_of(col_ref, step)
+            cols = columns_of(column_ref, step)
             for side in range(2):
                 weight = alphas_of(cols, along, downs[side]) * through[side]
                 through[side] = through[side] - weight
                 for c in range(3):
                     sums[side][c] = sums[side][c] + cols[6 + c] * weight
+        return through, sums
+
+    def draw_join(slot, carry, through, sums):
+        tile = tile_ref[slot]
+        fresh = (slot == 0) | (tile != tile_ref[jnp.maximum(slot - 1, 0)])
         after = []
         for side in range(2):
             start = jnp.where(fresh, 1.0, carry[side])
@@ -181,8 +202,14 @@
                 image_ref[tile, c : c + 1, lanes] = held + shade_sum
         return tuple(after)
 
+    def draw(pair, carry):
+        locals_two = [draw_local(2 * pair + k, col_ref.at[k]) for k in range(2)]
+        for k in range(2):
+            carry = draw_join(2 * pair + k, carry, *locals_two[k])
+        return carry
+
     ones = jnp.ones((1, HALF), jnp.float32)
-    lax.fori_loop(0, live, draw, (ones, ones))
+    lax.fori_loop(0, (live + 1) // 2, draw, (ones, ones))
     lane_tile = lax.broadcasted_iota(jnp.int32, (SEGMENTS, HALF), 1) // TILE_SIDE
     for side in range(2):
         lanes = slice(side * HALF, (side + 1) * HALF)
@@ -201,13 +228,14 @@
 
 def backward_kernel(
     tile_ref, info_ref, rec_ref, saved_ref, grad_ref, slots_ref, out_ref,
-    col_ref, weight_ref, pull_ref, block_ref, acc_ref,
+    col_ref, weight_ref, pull_ref, block_ref, acc_ref, wide_ref,
 ):
     live = info_ref[0]
     own = out_ref.shape[1]
     slots_total = rec_ref.shape[0]
     block_ref[...] = jnp.zeros_like(block_ref)
     acc_ref[...] = jnp.zeros_like(acc_ref)
+    fill_widener(wide_ref)
     along, downs = pixel_axes()
     seg_at = lax.broadcasted_iota(jnp.int32, (SEGMENTS, HALF), 0)
     rows16 = lax.broadcasted_iota(jnp.int32, (16, 2 * HALF), 0)
@@ -222,13 +250,13 @@
     basis = basis.astype(jnp.bfloat16)
     across = (((1,), (1,)), ((), ()))
 
-    def pull(turn, carry):
-        slot = live - 1 - turn
+    def pull_one(slot, carry, column_ref, heavy_ref, force_ref):
         tile = tile_ref[slot]
-        final = (turn == 0) | (tile != tile_ref[jnp.minimum(slot + 1, slots_total - 1)])
+        used = tile < TILES_DEV
+        final = (slot >= live - 1) | (tile != tile_ref[jnp.minimum(slot + 1, slots_total - 1)])
         rec = rec_ref[slot]
-        col_ref[...] = jnp.transpose(rec)
-        grads = grad_ref[tile]
+        widen(rec, wide_ref, column_ref)
+        grads = grad_ref[jnp.minimum(tile, TILES_DEV - 1)]
         after = []
         behind = []
         through = []
@@ -259,7 +287,7 @@
         alphas = [[], []]
         weights = [[], []]
         for step in range(STEPS):
-            cols = columns_of(col_ref, step)
+            cols = columns_of(column_ref, step)
             for side in range(2):
                 alpha = alphas_of(cols, along, downs[side])
                 weight = alpha * through[side]
@@ -267,28 +295,28 @@
                 alphas[side].append(alpha)
                 weights[side].append(weight)
                 lanes = slice(side * HALF, (side + 1) * HALF)
-                weight_ref[step * SEGMENTS : (step + 1) * SEGMENTS, lanes] = weight
+                heavy_ref[step * SEGMENTS : (step + 1) * SEGMENTS, lanes] = weight
         for step in reversed(range(STEPS)):
-            cols = columns_of(col_ref, step)
+            cols = columns_of(column_ref, step)
             for side in range(2):
                 lanes = slice(side * HALF, (side + 1) * HALF)
                 tints = colour_g[side]
                 lit = tints[0] * cols[6] + tints[1] * cols[7] + tints[2] * cols[8]
                 gap = lit - behind[side]
                 behind[side] = behind[side] + alphas[side][step] * gap
-                pull_ref[step * SEGMENTS : (step + 1) * SEGMENTS, lanes] = (
+                force_ref[step * SEGMENTS : (step + 1) * SEGMENTS, lanes] = (
                     weights[side][step] * gap
                 )
         found = lax.dot_general(
             basis,
-            jnp.concatenate(halves(pull_ref[...]), axis=0),
+            jnp.concatenate(halves(force_ref[...]), axis=0),
             across,
             preferred_element_type=jnp.float32,
         )
         moment = found[:, :BLOCK] + found[:, BLOCK:]
         painted = lax.dot_general(
             jnp.concatenate(halves(grads), axis=0),
-            jnp.concatenate(halves(weight_ref[...]), axis=0),
+            jnp.concatenate(halves(heavy_ref[...]), axis=0),
             across,
             preferred_element_type=jnp.float32,
         )
@@ -301,17 +329,23 @@
         h_xx = m_xx - 2.0 * at_x * m_x + at_x * at_x * m_0
         h_xy = m_xy - at_x * m_y - at_y * m_x + at_x * at_y * m_0
         h_yy = m_yy - 2.0 * at_y * m_y + at_y * at_y * m_0
-        block_ref[slot, 0:1, :] = -2.0 * con_a * h_x - con_b * h_y
-        block_ref[slot, 1:2, :] = -2.0 * con_c * h_y - con_b * h_x
-        block_ref[slot, 2:3, :] = -0.5 * h_xx
-        block_ref[slot, 3:4, :] = -h_xy
-        block_ref[slot, 4:5, :] = -0.5 * h_yy
-        block_ref[slot, 5:6, :] = (1.0 - open_s) * m_0
-        block_ref[slot, 6:9, :] = painted[0:3]
+        block_ref[slot, 0:1, :] = jnp.where(used, -2.0 * con_a * h_x - con_b * h_y, 0.0)
+        block_ref[slot, 1:2, :] = jnp.where(used, -2.0 * con_c * h_y - con_b * h_x, 0.0)
+        block_ref[slot, 2:3, :] = jnp.where(used, -0.5 * h_xx, 0.0)
+        block_ref[slot, 3:4, :] = jnp.where(used, -h_xy, 0.0)
+        block_ref[slot, 4:5, :] = jnp.where(used, -0.5 * h_yy, 0.0)
+        block_ref[slot, 5:6, :] = jnp.where(used, (1.0 - open_s) * m_0, 0.0)
+        block_ref[slot, 6:9, :] = jnp.where(used, painted[0:3], 0.0)
         return tuple(after)
 
+    def pull(turn, carry):
+        pair = (live + 1) // 2 - 1 - turn
+        for k in (1, 0):
+            carry = pull_one(2 * pair + k, carry, col_ref.at[k], weight_ref.at[k], pull_ref.at[k])
+        return carry
+
     zeros = jnp.zeros((1, HALF), jnp.float32)
-    lax.fori_loop(0, live, pull, (zeros, zeros))
+    lax.fori_loop(0, (live + 1) // 2, pull, (zeros, zeros))
 
     def spread(pair, carry):
         slots_row = slots_ref[pl.ds(pair, 1), :]
@@ -351,8 +385,9 @@
         scratch_shapes=[
             pltpu.VMEM((16, own), jnp.float32),
             pltpu.VMEM((48, own), jnp.bfloat16),
-            pltpu.VMEM((BLOCK, 16), jnp.float32),
-            pltpu.VMEM((TILES_DEV, 8, side), jnp.float32),
+            pltpu.VMEM((2, BLOCK, 9 * HALF), jnp.float32),
+            pltpu.VMEM((TILES_DEV + 1, 8, side), jnp.float32),
+            pltpu.VMEM((48, 9 * HALF), jnp.bfloat16),
         ],
         name="draw_tiles",
     )(tile_ids, info, received, pairs)
@@ -367,11 +402,12 @@
         in_specs=[smem(), smem(), vmem(), vmem(), vmem(), vmem()],
         out_specs=vmem(),
         scratch_shapes=[
-            pltpu.VMEM((BLOCK, 16), jnp.float32),
-            pltpu.VMEM((BLOCK, side), jnp.float32),
-            pltpu.VMEM((BLOCK, side), jnp.float32),
+            pltpu.VMEM((2, BLOCK, 9 * HALF), jnp.float32),
+            pltpu.VMEM((2, BLOCK, side), jnp.float32),
+            pltpu.VMEM((2, BLOCK, side), jnp.float32),
             pltpu.VMEM((slots_total, 16, BLOCK), jnp.float32),
             pltpu.VMEM((32, own), jnp.float32),
+            pltpu.VMEM((48, 9 * HALF), jnp.bfloat16),
         ],
         name="pull_tiles",
     )(tile_ids, info, recs, saved, grads, pairs)

time: 122 us -> 102 us (0.84)
  blocking collectives: 34 us -> 9.4 us
  Pallas kernels: 53 us -> 58.4 us
    all_to_all x1, blocking collectives: 34 us -> 9.4 us  [body(): lax.all_to_all(table_grad, 'gauss', split_axis=1, concat_axis=1, tiled=True)]
    pallas_call x1, Pallas kernels: 23.6 us -> 6.49 us  [exchange(): pl.pallas_call(functools.partial(halo_kernel, lax.axis_size('gauss'), lax...]
    pallas_call x1, Pallas kernels: 13.9 us -> 29.8 us  [pull_tiles(): pl.pallas_call(backward_kernel, out_shape=jax.ShapeDtypeStruct((9, own),...]
    pallas_call x1, Pallas kernels: 10.6 us -> 17.2 us  [draw_tiles(): pl.pallas_call(forward_kernel, out_shape=(jax.ShapeDtypeStruct((3, TILE_S...]
  transfers between devices with their start and end apart: 1 -> 1, of which waited for: 1 -> 1; matrix products, arithmetic and copies ran while one was open for 3% -> 4% of each run, Pallas kernels for 0% -> 0%
where the time goes in v3:
time: 102 us; the launch traced here: 101 us
  Pallas kernels  58.4 us (57%)
  local copies, waits for them, and re-layouts  12.7 us (12%)
  blocking collectives  9.4 us (9%)
  other arithmetic  8.92 us (9%)
  starting transfers between devices  7.39 us (7%)
  waiting for transfers between devices  2.92 us (3%)
    pallas_call x1, Pallas kernels, pull_tiles(): pl.pallas_call(backward_kernel, out_shape=jax.ShapeDtypeStruct((9, own),...  29.8 us
    pallas_call x1, Pallas kernels, draw_tiles(): pl.pallas_call(forward_kernel, out_shape=(jax.ShapeDtypeStruct((3, TILE_S...  17.2 us
    all_to_all x1, blocking collectives, body(): lax.all_to_all(table_grad, 'gauss', split_axis=1, concat_axis=1, tiled=True)  9.4 us
    all_to_all x1, starting transfers between devices, body(): lax.all_to_all(own_records[:, send_list], 'gauss', split_axis=1, concat_a...  7.39 us
    pallas_call x1, Pallas kernels, exchange(): pl.pallas_call(functools.partial(halo_kernel, lax.axis_size('gauss'), lax...  6.49 us
    pallas_call x1, Pallas kernels, ssim_pull(): pl.pallas_call(ssim_kernel, out_shape=jax.ShapeDtypeStruct((TILES_DEV, 8,...  4.9 us
    scatter x1, local copies, waits for them, and re-layouts, body(): own_grad = jnp.zeros_like(own_records).at[:, send_list].set(back_records)  3.21 us
    all_to_all x1, waiting for transfers between devices, body(): lax.all_to_all(own_records[:, send_list], 'gauss', split_axis=1, concat_a...  2.92 us
  transfers between devices with their start and end apart: 1, of which 1 were waited for; matrix products, arithmetic and copies ran while one was open for 4% of the time, Pallas kernels for 0%

profile of v3, /device:TPU:0, one launch (start us, length us, event | category | flops | bytes accessed | tf_op | source)
XLA Modules:
  0.0 100.5 jit_solution(13702534405561423100)
XLA Ops:
  0.6 0.0 copy-start.3
  0.6 0.0 copy-start.2
  0.7 0.8 slice.28
  1.4 0.9 multiply_multiply_fusion
  2.3 0.7 compare_select_fusion
  3.0 0.9 multiply_multiply_fusion.1
  3.9 0.1 stack.16
  4.0 1.0 multiply_reduce_fusion.1
  5.0 0.2 copy.38
  5.2 2.8 %gather_fusion = f32[1024,9]{1,0:T(8,128)S(1)} fusion(f32[9,1024]{0,1:T(8,128)S(1)} %copy.38, s32[1024]{0:T(1024)S(1)} %get-tuple-element.36), kind=kCustom, calls=%fused_computation | custom fusion | bytes 77824 | tf_op jit(solution)/shard_map/gather | solution.py:603
  8.1 0.2 copy.39
  8.3 0.7 reshape.57
  9.0 7.4 %all-to-all-start = ((f32[16,1,576]{2,1,0:T(1,128)}), f32[16,1,576]{2,1,0:T(1,128)S(1)}, u32[]{:S(2)}, u32[]{:S(2)}) async-start(f32[16,1,576]{2,1,0:T(1,128)} %reshape.57), calls=%async_computation | async-start | bytes 81920 | tf_op jit(solution)/shard_map/all_to_all | solution.py:602
  16.4 0.0 copy-done.3
  16.4 0.7 fusion.8
  17.1 0.0 copy-done.2
  17.1 0.1 copy.41
  17.2 0.2 copy.42
  17.5 0.8 reshape.35.slots_ref
  18.3 1.3 %pad_add_fusion.1.info_ref = s32[3]{0:T(128)} fusion(s32[1]{0:T(128)} %bitcast.3, s32[1]{0:T(128)} %bitcast.2, s32[1]{0:T(128)} %bitcast.1), kind=kLoop, calls=%fused_computation.55 | loop fusion | flops 6 | bytes 24 | tf_op jit(solution)/shard_map/stack | solution.py:609
  19.6 0.6 pad_add_fusion.2.place_ref
  20.2 2.9 %all-to-all-done = f32[16,1,576]{2,1,0:T(1,128)S(1)} async-done(((f32[16,1,576]{2,1,0:T(1,128)}), f32[16,1,576]{2,1,0:T(1,128)S(1)}, u32[]{:S(2)}, u32[]{:S(2)}) %all-to-all-start) | async-done | bytes 36896 | tf_op jit(solution)/shard_map/all_to_all | solution.py:602
  23.1 0.5 broadcast.272
  23.6 0.6 reduce
  24.2 0.1 reshape.58
  24.3 0.7 all_to_all.17.recv_ref
  25.1 17.2 %draw_tiles.1 = (f32[3,16,128]{2,1,0:T(8,128)}, f32[48,16,128]{2,1,0:T(8,128)}, f32[48,5,8,256]{3,2,1,0:T(8,128)}) custom-call(s32[48]{0:T(128)} %bitcast.47, s32[3]{0:T(128)} %pad_add_fusion.1.info_ref, f32[9,1024]{1,0:T(8,128)} %all_to_all.17.recv_ref, s32[24,256]{1,0:T(8,128)} %reshape.35.slots_ref), custom_call_target="tpu_custom_call" | custom-call | tf_op jit(solution)/shard_map/draw_tiles/pallas_call | solution.py:376
  42.3 6.5 %halo.1.wide_ref = f32[6,48,384]{2,1,0:T(8,128)} custom-call(f32[3,16,128]{2,1,0:T(8,128)} %get-tuple-element.12.shown_ref, f32[3,16,128]{2,1,0:T(8,128)} %target_ref.1), custom_call_target="tpu_custom_call" | custom-call | tf_op jit(solution)/shard_map/halo/pallas_call | solution.py:497
  48.8 4.9 %ssim_pull.1.grad_ref = f32[8,8,256]{2,1,0:T(8,128)} custom-call(s32[4]{0:T(128)} %pad_add_fusion.2.place_ref, f32[6,48,384]{2,1,0:T(8,128)} %halo.1.wide_ref), custom_call_target="tpu_custom_call" | custom-call | tf_op jit(solution)/shard_map/ssim_pull/pallas_call | solution.py:586
  53.7 29.8 %pull_tiles.1 = f32[9,1024]{1,0:T(8,128)} custom-call(s32[48]{0:T(128)} %bitcast.48, s32[3]{0:T(128)} %pad_add_fusion.1.info_ref, f32[48,16,128]{2,1,0:T(8,128)} %get-tuple-element.7.rec_ref, f32[48,5,8,256]{3,2,1,0:T(8,128)} %get-tuple-element.8.saved_ref, f32[8,8,256]{2,1,0:T(8,128)} %ssim_pull.1.grad_ref, s32[24,256]{1,0:T(8,128)} %reshape.35.slots_ref), custom_call_target="tpu_custom_call" | custom-call | tf_op jit(solution)/shard_map/pull_tiles/pallas_call | solution.py:399
  83.5 1.0 all_to_all.18
  84.5 0.1 reshape.59
  84.6 0.0 copy-start.1
  84.6 9.4 %all_to_all.23 = f32[16,1,576]{2,1,0:T(1,128)S(1)} all-to-all(f32[16,1,576]{2,1,0:T(1,128)S(1)} %reshape.59), channel_id=1, replica_groups=mesh['gauss'=16,'tile'=2] {'gauss'}, dimensions={0} | all-to-all | bytes 73728 | tf_op jit(solution)/shard_map/all_to_all | solution.py:622
  94.0 0.6 reduce.1
  94.6 0.1 reshape.60
  94.7 0.1 reshape.46
  94.8 0.2 copy.45
  95.1 3.2 %scatter_custom_fusion = f32[9,1024]{0,1:T(8,128)S(1)} fusion(s32[1024]{0:T(1024)S(1)} %get-tuple-element.35, f32[1024,9]{1,0:T(8,128)S(1)} %copy.45, f32[]{:T(128)} %constant.23.clone.1), kind=kCustom, calls=%fused_computation.2 | custom fusion | bytes 36868 | tf_op jit(solution)/shard_map/scatter | solution.py:623
  98.3 0.2 slice.37
  98.5 0.2 copy.46
  98.7 0.7 broadcast_multiply_fusion
  99.4 0.0 copy-done.1
  99.4 0.1 add_add_fusion
  99.5 0.1 add_add_fusion.1
  99.6 0.1 add_add_fusion.2
  99.7 0.2 copy.47
  99.9 0.6 pad_maximum_fusion.1
  (10 shorter events, 0.1 us)
Async XLA Ops:
  0.6 15.8 %copy-start.3 = (s32[1,48]{1,0:T(1,128)S(1)}, s32[1,48]{1,0:T(1,128)}, u32[]{:S(2)}) copy-start(s32[1,48]{1,0:T(1,128)} %param.10) | copy-start | bytes 580
  0.6 16.5 %copy-start.2 = (s32[1,48,128]{2,1,0:T(8,128)S(1)}, s32[1,48,128]{2,1,0:T(8,128)}, u32[]{:S(2)}) copy-start(s32[1,48,128]{2,1,0:T(8,128)} %param.9) | copy-start | bytes 73732
  9.0 14.1 %all-to-all-start = ((f32[16,1,576]{2,1,0:T(1,128)}), f32[16,1,576]{2,1,0:T(1,128)S(1)}, u32[]{:S(2)}, u32[]{:S(2)}) async-start(f32[16,1,576]{2,1,0:T(1,128)} %reshape.57), calls=%async_computation | async-start | bytes 81920 | tf_op jit(solution)/shard_map/all_to_all | solution.py:602
  83.5 15.2 %copy-start = (f32[48,1024]{1,0:T(8,128)S(1)}, f32[48,1024]{1,0:T(8,128)}, u32[]{:S(2)}) copy-start(f32[48,1024]{1,0:T(8,128)} %param.7) | copy-start | bytes 589828
  84.6 14.8 %copy-start.1 = (f32[9,1024]{1,0:T(8,128)S(1)}, f32[9,1024]{1,0:T(8,128)}, u32[]{:S(2)}) copy-start(f32[9,1024]{1,0:T(8,128)} %param.6) | copy-start | bytes 110596

commit v4 on v3

--- a/solution.py
+++ b/solution.py
@@ -360,6 +360,64 @@
 
     lax.fori_loop(0, (live + 1) // 2, spread, 0)
     out_ref[...] = acc_ref[0:9, :] + acc_ref[16:25, :]
+
+
+def pick_kernel(table_ref, list_ref, out_ref, pad_ref, split_ref):
+    own = table_ref.shape[1]
+    pad_ref[...] = jnp.zeros_like(pad_ref)
+    pad_ref[0:9, :] = table_ref[...]
+    for at, part in enumerate(thirds(pad_ref[...])):
+        split_ref[16 * at : 16 * (at + 1), :] = part
+
+    def one(turn, carry):
+        lanes = pl.ds(pl.multiple_of(turn * CHUNK, CHUNK), CHUNK)
+        wanted = list_ref[:, lanes]
+        found = jnp.zeros((48, CHUNK), jnp.float32)
+        for base in range(0, own, CHUNK):
+            found = found + jnp.dot(
+                split_ref[:, base : base + CHUNK],
+                selector(wanted, base, CHUNK),
+                preferred_element_type=jnp.float32,
+            )
+        out_ref[:, lanes] = (found[0:16] + found[16:32] + found[32:48])[0:9]
+        return carry
+
+    lax.fori_loop(0, own // CHUNK, one, 0)
+
+
+def place_kernel(table_ref, list_ref, out_ref, pad_ref, acc_ref):
+    own = table_ref.shape[1]
+    pad_ref[...] = jnp.zeros_like(pad_ref)
+    pad_ref[0:9, :] = table_ref[...]
+    acc_ref[...] = jnp.zeros_like(acc_ref)
+
+    def one(turn, carry):
+        lanes = pl.ds(pl.multiple_of(turn * CHUNK, CHUNK), CHUNK)
+        wanted = list_ref[:, lanes]
+        parts = jnp.concatenate(thirds(pad_ref[:, lanes]), axis=0)
+        for base in range(0, own, CHUNK):
+            acc_ref[:, base : base + CHUNK] += lax.dot_general(
+                parts,
+                selector(wanted, base, CHUNK),
+                (((1,), (1,)), ((), ())),
+                preferred_element_type=jnp.float32,
+            )
+        return carry
+
+    lax.fori_loop(0, own // CHUNK, one, 0)
+    out_ref[...] = acc_ref[0:9, :] + acc_ref[16:25, :] + acc_ref[32:41, :]
+
+
+def permuted(kernel, table, listed, scratch_type, name):
+    own = table.shape[1]
+    return pl.pallas_call(
+        kernel,
+        out_shape=jax.ShapeDtypeStruct(table.shape, jnp.float32),
+        in_specs=[vmem(), vmem()],
+        out_specs=vmem(),
+        scratch_shapes=[pltpu.VMEM((16, own), jnp.float32), pltpu.VMEM((48, own), scratch_type)],
+        name=name,
+    )(table, listed.reshape(1, own))
 
 
 def smem():
@@ -600,7 +658,7 @@
     peers = lax.axis_size("tile")
     own_records = jnp.concatenate([splats[0:6], shade(splats[6:9], sh_coeffs)], axis=0)
     received = lax.all_to_all(
-        own_records[:, send_list], "gauss", split_axis=1, concat_axis=1, tiled=True
+        permuted(pick_kernel, own_records, send_list, jnp.bfloat16, "pick"), "gauss", split_axis=1, concat_axis=1, tiled=True
     )
     tile_ids = block_tiles[0]
     slot_rows = block_slots[0]
@@ -620,7 +678,7 @@
     tile_grad = ssim_pull(place, exchange(rendered, target))
     table_grad = pull_tiles(tile_ids, info, recs, saved, tile_grad, pairs, received.shape[1])
     back_records = lax.all_to_all(table_grad, "gauss", split_axis=1, concat_axis=1, tiled=True)
-    own_grad = jnp.zeros_like(own_records).at[:, send_list].set(back_records)
+    own_grad = permuted(place_kernel, back_records, send_list, jnp.float32, "place")
     unused_colour, shade_pull = jax.vjp(shade, splats[6:9], sh_coeffs)
     dir_grad, grad_sh = shade_pull(own_grad[6:9])
     grad_splats = jnp.concatenate([own_grad[0:6], dir_grad], axis=0)

time: 102 us -> 104 us (1.020); the launches traced: 101 us -> 104 us
  Pallas kernels: 58.4 us -> 64 us
  local copies, waits for them, and re-layouts: 12.7 us -> 9.24 us
  blocking collectives: 9.4 us -> 11.2 us
  waiting for transfers between devices: 2.92 us -> 1.53 us
    pallas_call x0 -> x2, Pallas kernels: none -> 5.03 us  [permuted(): pl.pallas_call(kernel, out_shape=jax.ShapeDtypeStruct(table.shape, jnp.fl...]
    scatter x1 -> x0, local copies, waits for them, and re-layouts: 3.21 us -> none  [body(): own_grad = jnp.zeros_like(own_records).at[:, send_list].set(back_records)]
    gather x1 -> x0, local copies, waits for them, and re-layouts: 2.81 us -> none  [body(): own_records[:, send_list]]
    all_to_all x1, blocking collectives: 9.4 us -> 11.2 us  [body(): lax.all_to_all(table_grad, 'gauss', split_axis=1, concat_axis=1, tiled=True)]
    all_to_all x1, waiting for transfers between devices: 2.92 us -> 1.53 us  [body(): lax.all_to_all(permuted(pick_kernel, own_records, send_list, jnp.bfloat16...]
    all_to_all x4 -> x5, local copies, waits for them, and re-layouts: 1.44 us -> 2.17 us  [body(): lax.all_to_all(permuted(pick_kernel, own_records, send_list, jnp.bfloat16...]
  transfers between devices with their start and end apart: 1 -> 1, of which waited for: 1 -> 1; matrix products, arithmetic and copies ran while one was open for 4% -> 5% of each run, Pallas kernels for 0% -> 0%
where the time goes in v4:
time: 104 us
  Pallas kernels  64 us (62%)
  blocking collectives  11.2 us (11%)
  other arithmetic  9.5 us (9%)
  local copies, waits for them, and re-layouts  9.24 us (9%)
  starting transfers between devices  7.39 us (7%)
  waiting for transfers between devices  1.53 us (1%)
    pallas_call x1, Pallas kernels, pull_tiles(): pl.pallas_call(backward_kernel, out_shape=jax.ShapeDtypeStruct((9, own),...  29.9 us
    pallas_call x1, Pallas kernels, draw_tiles(): pl.pallas_call(forward_kernel, out_shape=(jax.ShapeDtypeStruct((3, TILE_S...  17.2 us
    all_to_all x1, blocking collectives, body(): lax.all_to_all(table_grad, 'gauss', split_axis=1, concat_axis=1, tiled=True)  11.2 us
    all_to_all x1, starting transfers between devices, body(): lax.all_to_all(permuted(pick_kernel, own_records, send_list, jnp.bfloat16...  7.39 us
    pallas_call x1, Pallas kernels, exchange(): pl.pallas_call(functools.partial(halo_kernel, lax.axis_size('gauss'), lax...  7.01 us
    pallas_call x2, Pallas kernels, permuted(): pl.pallas_call(kernel, out_shape=jax.ShapeDtypeStruct(table.shape, jnp.fl...  5.03 us
    pallas_call x1, Pallas kernels, ssim_pull(): pl.pallas_call(ssim_kernel, out_shape=jax.ShapeDtypeStruct((TILES_DEV, 8,...  4.9 us
    all_to_all x5, local copies, waits for them, and re-layouts, body(): lax.all_to_all(permuted(pick_kernel, own_records, send_list, jnp.bfloat16...  2.17 us
  transfers between devices with their start and end apart: 1, of which 1 were waited for; matrix products, arithmetic and copies ran while one was open for 5% of the time, Pallas kernels for 0%

profile of v4, /device:TPU:0, one launch (start us, length us, event | category | flops | bytes accessed | tf_op | source)
XLA Modules:
  0.0 103.6 jit_solution(12927643092730089310)
XLA Ops:
  0.6 0.8 slice.28
  1.4 0.9 multiply_multiply_fusion
  2.3 0.9 multiply_multiply_fusion.1
  3.2 0.1 stack.16
  3.3 1.0 multiply_reduce_fusion.1
  4.3 0.6 pad_maximum_fusion.table_ref
  4.9 2.3 %pick.1 = f32[9,1024]{1,0:T(8,128)} custom-call(f32[9,1024]{1,0:T(8,128)} %pad_maximum_fusion.table_ref, s32[1,1024]{1,0:T(1,128)} %bitcast.41), custom_call_target="tpu_custom_call" | custom-call | tf_op jit(solution)/shard_map/pick/pallas_call | solution.py:413
  7.3 0.9 all_to_all.14
  8.2 0.7 reshape.42
  8.9 7.4 %all-to-all-start = ((f32[16,1,576]{2,1,0:T(1,128)}), f32[16,1,576]{2,1,0:T(1,128)S(1)}, u32[]{:S(2)}, u32[]{:S(2)}) async-start(f32[16,1,576]{2,1,0:T(1,128)} %reshape.42), calls=%async_computation | async-start | bytes 81920 | tf_op jit(solution)/shard_map/all_to_all | solution.py:660
  16.3 1.4 %fusion.6 = s32[]{:T(128)} fusion(s32[1,48]{1,0:T(1,128)} %param.10), kind=kLoop, calls=%fused_computation.48 | loop fusion | flops 143 | bytes 196 | tf_op jit(solution)/shard_map/reduce_sum | solution.py:666
  17.7 0.8 copy.14
  18.5 0.2 copy.15
  18.8 0.8 reshape.40.slots_ref
  19.6 1.3 %pad_add_fusion.1.info_ref = s32[3]{0:T(128)} fusion(s32[1]{0:T(128)} %bitcast.3, s32[1]{0:T(128)} %bitcast.2, s32[1]{0:T(128)} %bitcast.1), kind=kLoop, calls=%fused_computation.49 | loop fusion | flops 6 | bytes 24 | tf_op jit(solution)/shard_map/stack | solution.py:667
  20.9 0.6 pad_add_fusion.2.place_ref
  21.5 1.5 %all-to-all-done = f32[16,1,576]{2,1,0:T(1,128)S(1)} async-done(((f32[16,1,576]{2,1,0:T(1,128)}), f32[16,1,576]{2,1,0:T(1,128)S(1)}, u32[]{:S(2)}, u32[]{:S(2)}) %all-to-all-start) | async-done | bytes 36896 | tf_op jit(solution)/shard_map/all_to_all | solution.py:660
  23.0 0.5 broadcast.254
  23.5 0.6 reduce
  24.1 0.1 reshape.43
  24.2 0.7 all_to_all.16.recv_ref
  25.0 17.2 %draw_tiles.1 = (f32[3,16,128]{2,1,0:T(8,128)}, f32[48,16,128]{2,1,0:T(8,128)}, f32[48,5,8,256]{3,2,1,0:T(8,128)}) custom-call(s32[48]{0:T(128)} %bitcast.43, s32[3]{0:T(128)} %pad_add_fusion.1.info_ref, f32[9,1024]{1,0:T(8,128)} %all_to_all.16.recv_ref, s32[24,256]{1,0:T(8,128)} %reshape.40.slots_ref), custom_call_target="tpu_custom_call" | custom-call | tf_op jit(solution)/shard_map/draw_tiles/pallas_call | solution.py:434
  42.2 7.0 %halo.1.wide_ref = f32[6,48,384]{2,1,0:T(8,128)} custom-call(f32[3,16,128]{2,1,0:T(8,128)} %get-tuple-element.3.shown_ref, f32[3,16,128]{2,1,0:T(8,128)} %target_ref.1), custom_call_target="tpu_custom_call" | custom-call | tf_op jit(solution)/shard_map/halo/pallas_call | solution.py:555
  49.2 4.9 %ssim_pull.1.grad_ref = f32[8,8,256]{2,1,0:T(8,128)} custom-call(s32[4]{0:T(128)} %pad_add_fusion.2.place_ref, f32[6,48,384]{2,1,0:T(8,128)} %halo.1.wide_ref), custom_call_target="tpu_custom_call" | custom-call | tf_op jit(solution)/shard_map/ssim_pull/pallas_call | solution.py:644
  54.1 0.0 copy-start
  54.1 0.0 copy-start.1
  54.1 29.9 %pull_tiles.1 = f32[9,1024]{1,0:T(8,128)} custom-call(s32[48]{0:T(128)} %bitcast.44, s32[3]{0:T(128)} %pad_add_fusion.1.info_ref, f32[48,16,128]{2,1,0:T(8,128)} %get-tuple-element.7.rec_ref, f32[48,5,8,256]{3,2,1,0:T(8,128)} %get-tuple-element.8.saved_ref, f32[8,8,256]{2,1,0:T(8,128)} %ssim_pull.1.grad_ref, s32[24,256]{1,0:T(8,128)} %reshape.40.slots_ref), custom_call_target="tpu_custom_call" | custom-call | tf_op jit(solution)/shard_map/pull_tiles/pallas_call | solution.py:457
  84.0 0.9 all_to_all.17
  84.9 0.1 reshape.44
  85.0 11.2 %all_to_all.22 = f32[16,1,576]{2,1,0:T(1,128)S(1)} all-to-all(f32[16,1,576]{2,1,0:T(1,128)S(1)} %reshape.44), channel_id=1, replica_groups=mesh['gauss'=16,'tile'=2] {'gauss'}, dimensions={0} | all-to-all | bytes 73728 | tf_op jit(solution)/shard_map/all_to_all | solution.py:680
  96.2 0.6 reduce.1
  96.8 0.1 reshape.45
  96.9 0.7 all_to_all.19.table_ref
  97.6 2.7 %place.1 = f32[9,1024]{1,0:T(8,128)} custom-call(f32[9,1024]{1,0:T(8,128)} %all_to_all.19.table_ref, s32[1,1024]{1,0:T(1,128)} %bitcast.42), custom_call_target="tpu_custom_call" | custom-call | tf_op jit(solution)/shard_map/place/pallas_call | solution.py:413
  100.3 0.8 slice.35
  101.2 0.8 slice.34
  101.9 0.0 copy-done
  101.9 0.7 broadcast_multiply_fusion
  102.6 0.0 copy-done.1
  102.6 0.1 add_add_fusion
  102.7 0.1 add_add_fusion.1
  102.8 0.1 add_add_fusion.2
  102.9 0.6 pad_maximum_fusion.1
  (8 shorter events, 0.1 us)
Async XLA Ops:
  8.9 14.1 %all-to-all-start = ((f32[16,1,576]{2,1,0:T(1,128)}), f32[16,1,576]{2,1,0:T(1,128)S(1)}, u32[]{:S(2)}, u32[]{:S(2)}) async-start(f32[16,1,576]{2,1,0:T(1,128)} %reshape.42), calls=%async_computation | async-start | bytes 81920 | tf_op jit(solution)/shard_map/all_to_all | solution.py:660
  54.1 47.8 %copy-start = (f32[48,1024]{1,0:T(8,128)S(1)}, f32[48,1024]{1,0:T(8,128)}, u32[]{:S(2)}) copy-start(f32[48,1024]{1,0:T(8,128)} %param.7) | copy-start | bytes 589828
  54.1 48.5 %copy-start.1 = (f32[9,1024]{1,0:T(8,128)S(1)}, f32[9,1024]{1,0:T(8,128)}, u32[]{:S(2)}) copy-start(f32[9,1024]{1,0:T(8,128)} %param.6) | copy-start | bytes 110596
